TPU v7x, 512 devices: a whole 4x4x16 slice. The times are simulated.
512 devices in a mesh: ctx: 16 (over y, z_hi, core), row: 4 (over x), col: 8 (over z_lo).
Axes of the slice: x: 4, y: 4, z: 16 (z_hi: 2, z_lo: 8; z = z_hi * 8 + z_lo), core: 2. Of those that a mesh axis runs over, the one named last changes fastest.
Arguments:
- patches: bfloat16 [12288, 2048], P(('ctx', 'row'), 'col'), may hold values from -6 to 6
- visible: int32 [12288], P(('ctx', 'row')), may hold values from -1 to 262143, as said below
- ln_gain: float32 [2048], replicated, may hold values from 0.1 to 1.9
- ln_bias: float32 [2048], replicated, may hold values from -3 to 3
- w_query: bfloat16 [2048, 2048], P('row', 'col')
- w_key: bfloat16 [2048, 2048], P('row', 'col')
- w_value: bfloat16 [2048, 2048], P('row', 'col'), may hold values from -0.125 to 0.125
- w_output: bfloat16 [2048, 2048], P('row', 'col'), may hold values from -0.375 to 0.375
Outputs:
- attn_out: float32 [12288, 2048], P(('ctx', 'row'), 'col')
Inputs may be any that keep to these rules, and one draw needn't show every extreme that they name: Slots s * 768 to (s + 1) * 768 - 1 form slab s: first the distinct visible patch numbers of that slab in increasing order, all in s * 16384 to (s + 1) * 16384 - 1, then -1 in every remaining slot. Each slab holds 384 or more visible patches, and some slab is full.
All inputs are finite; a program needn't handle non-finite values.
Results may differ from a plain program's by a relative error of at most 0.0094.
Values may be sent and summed in bfloat16 or wider, within the bound.
No kernel may reach another device: no remote copies, remote signals or barrier semaphores. Data moves between devices by JAX's collectives and lax.ppermute only.
A program may use at most 128 MiB of HBM per device.

v0:
```python
import math

import jax
import jax.numpy as jnp
from jax import lax
from jax.experimental import pallas as pl
from jax.experimental.pallas import tpu as pltpu
from jax.sharding import Mesh
from jax.sharding import PartitionSpec as P


HEAD_DIM = 128
GRID = 64
ROWS = 192
F32 = jnp.float32
BF16 = jnp.bfloat16
SHIFTS = (0, 1, 3, 2)


def embed(visible, full_width):
    patch_id = jnp.maximum(visible, 0)
    plane_size = GRID * GRID
    coord_x = (patch_id // plane_size).astype(F32)
    coord_y = (patch_id // GRID % GRID).astype(F32)
    coord_z = (patch_id % GRID).astype(F32)
    channel = jnp.arange(full_width, dtype=jnp.int32)
    axis_pick = channel % 3
    frequency = jnp.exp(-math.log(10000.0) * (channel // 6 * 6).astype(F32) / full_width)
    offset_phase = 0.5 * math.pi * (channel // 3 % 2).astype(F32)
    picked = jnp.where(
        axis_pick[None, :] == 0,
        coord_x[:, None],
        jnp.where(axis_pick[None, :] == 1, coord_y[:, None], coord_z[:, None]),
    )
    return jnp.sin(picked * frequency[None, :] + offset_phase[None, :])


def spread(block, axes, count):
    copies = jnp.broadcast_to(block[None], (count,) + block.shape)
    return lax.all_to_all(copies, axes, 0, 0)


def ring(count, shift):
    return [(i, (i + shift) % count) for i in range(count)]


def norm_kernel(par_ref, near_ref, side_ref, pos_ref, gain_ref, bias_ref, out_ref):
    step = 64
    even = par_ref[0] == 0
    for r in range(0, ROWS, step):
        rows = slice(r, r + step)
        parts = []
        for z in range(8):
            near = near_ref[z // 2, rows, :]
            side = side_ref[z // 2, rows, :]
            mine = jnp.where(even == (z % 2 == 0), near, side)
            parts.append(mine.astype(F32) + pos_ref[rows, z * 256 : (z + 1) * 256])
        total = sum(jnp.sum(p, axis=1, keepdims=True) for p in parts)
        mean = total * (1.0 / 2048)
        parts = [p - mean for p in parts]
        square = sum(jnp.sum(p * p, axis=1, keepdims=True) for p in parts)
        scale = lax.rsqrt(square * (1.0 / 2048) + 1e-06)
        for z in range(8):
            lanes = slice(z * 256, (z + 1) * 256)
            value = parts[z] * scale * gain_ref[:, lanes] + bias_ref[:, lanes]
            out_ref[z // 2, rows, (z % 2) * 256 : (z % 2 + 1) * 256] = value.astype(BF16)


def qkv_kernel(
    src_ref, core_ref, own_ref, oth_ref, w0_ref, w1_ref, w2_ref, w3_ref, cnt_ref, q_ref, kv_ref, kvs_ref
):
    for c, n_ref in enumerate((own_ref, oth_ref)):
        acc = jnp.zeros((ROWS, 384), F32)
        for s, w_ref in enumerate((w0_ref, w1_ref, w2_ref, w3_ref)):
            acc = acc + jnp.dot(n_ref[src_ref[s]], w_ref[:, :384], preferred_element_type=F32)
        at = pl.multiple_of((core_ref[0] ^ c) * ROWS, ROWS)
        query = (acc[:, :128] * (1.0 / math.sqrt(HEAD_DIM))).astype(BF16)
        pair = acc[:, 128:384].astype(BF16)
        count = cnt_ref[c].astype(BF16)
        for copy in range(4):
            q_ref[copy, pl.ds(at, ROWS), :] = query
            kvs_ref[copy, c, :ROWS, :] = pair
            kvs_ref[copy, c, ROWS:, :] = count
        kv_ref[c, :ROWS, :] = pair
        kv_ref[c, ROWS:, :] = count


NT = (((1,), (1,)), ((), ()))
TN = (((0,), (0,)), ((), ()))


def scan_keys(query, kv_ref, s_ref, acc_ref, best, total):
    width = query.shape[0]
    blocks = kv_ref.shape[0]
    before = best

    def first(b, best):
        for c in range(2):
            keys = kv_ref[b, c, :ROWS, :128]
            score = lax.dot_general(keys, query, NT, preferred_element_type=F32)
            row = lax.broadcasted_iota(jnp.int32, (ROWS, width), 0).astype(F32)
            live = kv_ref[b, c, pl.ds(ROWS, 1), :].astype(F32)
            live = jnp.concatenate([live] * (width // 256), axis=1)
            score = jnp.where(row < live, score, -1e30)
            s_ref[pl.ds((b * 2 + c) * ROWS, ROWS), :] = score
            best = jnp.maximum(best, jnp.max(score, axis=0, keepdims=True))
        return best

    best = lax.fori_loop(0, blocks, first, best)
    shrink = jnp.exp(before - best)
    total = total * shrink
    acc_ref[...] = acc_ref[...] * shrink

    def second(b, total):
        for c in range(2):
            weight = jnp.exp(s_ref[pl.ds((b * 2 + c) * ROWS, ROWS), :] - best)
            total = total + jnp.sum(weight, axis=0, keepdims=True)
            values = kv_ref[b, c, :ROWS, 128:256]
            acc_ref[...] += lax.dot_general(
                values, weight.astype(BF16), TN, preferred_element_type=F32
            )
        return total

    return best, lax.fori_loop(0, blocks, second, total)


def near_kernel(q_ref, kv_ref, acc_ref, stat_ref, s_ref):
    width = q_ref.shape[0]
    acc_ref[...] = jnp.zeros_like(acc_ref)
    best, total = scan_keys(
        q_ref[...],
        kv_ref,
        s_ref,
        acc_ref,
        jnp.full((1, width), -1e30, F32),
        jnp.zeros((1, width), F32),
    )
    stat_ref[0:1, :] = best
    stat_ref[1:2, :] = total
    stat_ref[2:8, :] = jnp.zeros((6, width), F32)


def far_kernel(q_ref, kv_ref, part_ref, stat_ref, out_ref, s_ref, acc_ref):
    width = q_ref.shape[0]
    acc_ref[...] = part_ref[...]
    best, total = scan_keys(
        q_ref[...], kv_ref, s_ref, acc_ref, stat_ref[0:1, :], stat_ref[1:2, :]
    )
    mixed = (acc_ref[...] / total).T.astype(BF16)
    level = best + jnp.log(total)
    high = level.astype(BF16)
    rest = level - high.astype(F32)
    mid = rest.astype(BF16)
    low = (rest - mid.astype(F32)).astype(BF16)
    for x in range(width // (2 * ROWS)):
        stats = []
        for part in (high, mid, low):
            for piece in range(3):
                at = x * 2 * ROWS + piece * 128
                stats.append(part[:, at : at + 128].astype(F32))
        stats.append(jnp.zeros((7, 128), F32))
        stats = jnp.concatenate(stats, axis=0).astype(BF16)
        for c in range(2):
            at = (2 * x + c) * ROWS
            out_ref[2 * x + c, :ROWS, :] = mixed[at : at + ROWS, :]
            out_ref[2 * x + c, ROWS : ROWS + 16, :] = stats


def out_kernel(src_ref, par_ref, near_ref, side_ref, w0_ref, w1_ref, w2_ref, w3_ref, out_ref):
    acc = jnp.zeros(out_ref.shape, F32)
    for s, w_ref in enumerate((w0_ref, w1_ref, w2_ref, w3_ref)):
        for flip, m_ref in enumerate((near_ref, side_ref)):
            at = pl.multiple_of((par_ref[0] ^ flip) * 256, 256)
            acc = acc + jnp.dot(
                m_ref[src_ref[s]], w_ref[pl.ds(at, 256), 384:640], preferred_element_type=F32
            )
    out_ref[...] = acc


VMEM = pl.BlockSpec(memory_space=pltpu.VMEM)
SMEM = pl.BlockSpec(memory_space=pltpu.SMEM)
PARAMS = pltpu.CompilerParams(vmem_limit_bytes=20 * 1024 * 1024)


def sublayer(patches, visible, ln_gain, ln_bias, w_query, w_key, w_value, w_output):
    core = lax.axis_index("core")
    row = lax.axis_index("row")
    lane = core * HEAD_DIM
    w_own = jnp.concatenate(
        [lax.dynamic_slice_in_dim(w, lane, HEAD_DIM, 1) for w in (w_query, w_key, w_value)]
        + [w_output],
        axis=1,
    )
    weights = [w_own]
    weights += [lax.ppermute(w_own, "row", ring(4, s)) for s in SHIFTS[1:]]
    source = jnp.stack([(row - s) % 4 for s in SHIFTS]).astype(jnp.int32)
    core = core.astype(jnp.int32)[None]
    parity = lax.axis_index("c0").astype(jnp.int32)[None]

    live = jnp.full((16, 256), jnp.sum((visible >= 0).astype(F32)), F32)
    counts = jnp.stack([live, lax.ppermute(live, "core", ring(2, 1))])

    pos = embed(visible, 2048)
    near = spread(patches, ("c2", "c1"), 4)
    near, weights, counts = lax.optimization_barrier((near, weights, counts))
    side = lax.ppermute(near, "c0", ring(2, 1))
    own = pl.pallas_call(
        norm_kernel,
        out_shape=jax.ShapeDtypeStruct((4, ROWS, 512), BF16),
        in_specs=[SMEM] + [VMEM] * 5,
        out_specs=VMEM,
        compiler_params=PARAMS,
        name="norm",
    )(parity, near, side, pos, ln_gain[None, :], ln_bias[None, :])
    other = lax.ppermute(own, "core", ring(2, 1))
    query, kv, near_kv = pl.pallas_call(
        qkv_kernel,
        out_shape=(
            jax.ShapeDtypeStruct((4, 2 * ROWS, 128), BF16),
            jax.ShapeDtypeStruct((2, ROWS + 16, 256), BF16),
            jax.ShapeDtypeStruct((4, 2, ROWS + 16, 256), BF16),
        ),
        in_specs=[SMEM] * 2 + [VMEM] * 7,
        out_specs=(VMEM, VMEM, VMEM),
        compiler_params=PARAMS,
        name="qkv",
    )(source, core, own, other, *weights, counts)
    far_kv = lax.ppermute(kv, ("zh", "c2", "c1", "c0"), ring(16, 8))
    query = lax.all_to_all(query, "row", 0, 0).reshape(8 * ROWS, 128)
    near_kv = lax.all_to_all(near_kv, "y", 0, 0)
    far_kv, _ = lax.optimization_barrier((far_kv, near_kv))
    far_kv = spread(far_kv, "y", 4)
    kv_spec = pl.BlockSpec((4, 2, ROWS + 16, 256), lambda i: (0, 0, 0, 0))
    q_spec = pl.BlockSpec((4 * ROWS, 128), lambda i: (i, 0))
    acc_spec = pl.BlockSpec((128, 4 * ROWS), lambda i: (0, i))
    stat_spec = pl.BlockSpec((8, 4 * ROWS), lambda i: (0, i))
    acc, stat = pl.pallas_call(
        near_kernel,
        grid=(2,),
        out_shape=(
            jax.ShapeDtypeStruct((128, 8 * ROWS), F32),
            jax.ShapeDtypeStruct((8, 8 * ROWS), F32),
        ),
        in_specs=[q_spec, kv_spec],
        out_specs=(acc_spec, stat_spec),
        scratch_shapes=[pltpu.VMEM((8 * ROWS, 4 * ROWS), F32)],
        compiler_params=PARAMS,
        name="near",
    )(query, near_kv)
    part = pl.pallas_call(
        far_kernel,
        grid=(2,),
        out_shape=jax.ShapeDtypeStruct((8, ROWS + 16, 128), BF16),
        in_specs=[q_spec, kv_spec, acc_spec, stat_spec],
        out_specs=pl.BlockSpec((4, ROWS + 16, 128), lambda i: (i, 0, 0)),
        scratch_shapes=[
            pltpu.VMEM((8 * ROWS, 4 * ROWS), F32),
            pltpu.VMEM((128, 4 * ROWS), F32),
        ],
        compiler_params=PARAMS,
        name="far",
    )(query, far_kv, acc, stat)
    part = lax.all_to_all(part, ("row", "core"), 0, 0).reshape(4, 2, ROWS + 16, 128)
    stats = part[:, :, ROWS : ROWS + 9, :].astype(F32).reshape(4, 2, 3, 2 * ROWS).sum(axis=2)
    stats = lax.dynamic_slice_in_dim(stats, core[0] * ROWS, ROWS, 2)
    share = jnp.exp(stats - jnp.max(stats, axis=0, keepdims=True))
    share = share / jnp.sum(share, axis=0, keepdims=True)
    mixed = jnp.sum(part[:, :, :ROWS, :].astype(F32) * share[..., None], axis=0)
    mixed = jnp.concatenate([mixed[0], mixed[1]], axis=1).astype(BF16)
    near = spread(mixed, ("c2", "c1"), 4)
    side = lax.ppermute(near, "c0", ring(2, 1))
    return pl.pallas_call(
        out_kernel,
        out_shape=jax.ShapeDtypeStruct((ROWS, 256), F32),
        in_specs=[SMEM] * 2 + [VMEM] * 6,
        out_specs=VMEM,
        compiler_params=PARAMS,
        name="out",
    )(source, parity, near, side, *weights)


def solution(mesh):
    fine = Mesh(
        mesh.devices.reshape(4, 2, 2, 4, 2, 2, 2), ("y", "zh", "core", "row", "c2", "c1", "c0")
    )
    tokens = ("y", "zh", "core", "row")
    col = ("c2", "c1", "c0")
    placed = (
        P(tokens, col),
        P(tokens),
        P(),
        P(),
        P("row", col),
        P("row", col),
        P("row", col),
        P("row", col),
    )
    return jax.shard_map(
        sublayer, mesh=fine, in_specs=placed, out_specs=P(tokens, col), check_vma=False
    )
```

profile of v0, /device:TPU:1, one launch (start us, length us, event | category | flops | bytes accessed | tf_op | source)
XLA Modules:
  0.0 206.2 jit_solution(6404876393655446648)
XLA Ops:
  0.0 0.0 copy-start
  0.0 0.0 copy-start.12
  0.0 1.8 broadcast_in_dim.85
  1.8 11.8 %all-to-all-start = ((bf16[4,192,256]{2,1,0:T(8,128)(2,1)}), bf16[4,192,256]{2,1,0:T(8,128)(2,1)S(1)}, u32[]{:S(2)}, u32[]{:S(2)}) async-start(bf16[4,192,256]{2,1,0:T(8,128)(2,1)} %broadcast_in_dim.85), calls=%async_computation | async-start | bytes 786432 | tf_op jit(solution)/shard_map/all_to_all | solution.py:40
  13.6 0.0 copy-done
  13.6 0.0 copy-done.14
  13.6 0.0 copy-done.13
  13.7 0.0 copy-start.10
  13.7 0.0 copy-start.11
  13.7 0.0 copy-done.12
  13.7 0.1 pad_maximum_fusion.w0_ref
  13.8 3.1 %collective-permute-start = (bf16[512,640]{1,0:T(8,128)(2,1)S(1)}, bf16[512,640]{1,0:T(8,128)(2,1)S(1)}, u32[]{:S(2)}, u32[]{:S(2)}) collective-permute-start(bf16[512,640]{1,0:T(8,128)(2,1)S(1)} %pad_maximum_fusion.w0_ref), channel_id=1, source_target_pairs={{0,8},{8,16},{16,24},{24,0},{1,9},{9,17},{17,25},{25,1},{2,10},{10... | collective-permute-start | bytes 1966088 | tf_op jit(solution)/shard_map/ppermute | solution.py:195
  16.9 3.4 %collective-permute-start.1 = (bf16[512,640]{1,0:T(8,128)(2,1)S(1)}, bf16[512,640]{1,0:T(8,128)(2,1)S(1)}, u32[]{:S(2)}, u32[]{:S(2)}) collective-permute-start(bf16[512,640]{1,0:T(8,128)(2,1)S(1)} %pad_maximum_fusion.w0_ref), channel_id=1, source_target_pairs={{0,24},{8,0},{16,8},{24,16},{1,25},{9,1},{17,9},{25,17},{2,26},{10... | collective-permute-start | bytes 1966088 | tf_op jit(solution)/shard_map/ppermute | solution.py:195
  20.3 3.4 %collective-permute-start.2 = (bf16[512,640]{1,0:T(8,128)(2,1)S(1)}, bf16[512,640]{1,0:T(8,128)(2,1)S(1)}, u32[]{:S(2)}, u32[]{:S(2)}) collective-permute-start(bf16[512,640]{1,0:T(8,128)(2,1)S(1)} %pad_maximum_fusion.w0_ref), channel_id=1, source_target_pairs={{0,16},{8,24},{16,0},{24,8},{1,17},{9,25},{17,1},{25,9},{2,18},{10... | collective-permute-start | bytes 1966088 | tf_op jit(solution)/shard_map/ppermute | solution.py:195
  23.8 0.0 copy-done.15
  23.8 0.6 fusion.17
  24.4 0.6 broadcast_in_dim.86
  25.0 3.7 %collective-permute-start.3 = (f32[16,256]{1,0:T(8,128)S(1)}, f32[16,256]{1,0:T(8,128)S(1)}, u32[]{:S(2)}, u32[]{:S(2)}) collective-permute-start(f32[16,256]{1,0:T(8,128)S(1)} %broadcast_in_dim.86), channel_id=1, source_target_pairs={{0,32},{32,0},{1,33},{33,1},{2,34},{34,2},{3,35},{35,3},{4,36},{36... | collective-permute-start | bytes 49160 | tf_op jit(solution)/shard_map/ppermute | solution.py:201
  28.8 0.8 collective-permute-done.3
  29.6 0.6 stack.27.cnt_ref
  30.2 2.0 collective-permute-done.w1_ref
  32.3 1.6 collective-permute-done.1.w2_ref
  33.9 13.4 %collective-permute-done.2.w3_ref = bf16[512,640]{1,0:T(8,128)(2,1)S(1)} collective-permute-done((bf16[512,640]{1,0:T(8,128)(2,1)S(1)}, bf16[512,640]{1,0:T(8,128)(2,1)S(1)}, u32[]{:S(2)}, u32[]{:S(2)}) %collective-permute-start.2) | collective-permute-done | bytes 655392 | tf_op jit(solution)/shard_map/ppermute | solution.py:195
  47.3 0.8 copy-done.5
  48.1 0.0 all-to-all-done.near_ref
  48.1 3.5 %collective-permute-start.4 = (bf16[4,192,256]{2,1,0:T(8,128)(2,1)S(1)}, bf16[4,192,256]{2,1,0:T(8,128)(2,1)S(1)}, u32[]{:S(2)}, u32[]{:S(2)}) collective-permute-start(bf16[4,192,256]{2,1,0:T(8,128)(2,1)S(1)} %all-to-all-done.near_ref), channel_id=1, source_target_pairs={{0,1},{1,0},{2,3},{3,2},{4,5},{5,4},{6,7},{7,6},{8,9},{9,8},{10,11... | collective-permute-start | bytes 1179656 | tf_op jit(solution)/shard_map/ppermute | solution.py:206
  51.7 5.3 %add_sine_fusion.pos_ref = f32[192,2048]{1,0:T(8,128)S(1)} fusion(f32[2048]{0:T(1024)S(1)} %get-tuple-element.37, f32[2048]{0:T(1024)S(1)} %get-tuple-element.36, f32[192]{0:T(256)S(1)} %get-tuple-element.33, f32[192]{0:T(256)S(1)} %get-tuple-element.32, f32[192]{0:T(256)S(1)} %get-tuple-element.31, pred[2048]{0:T(1024)(128)(4,1)S(1)} %get-tuple-element.38, ...), kind=kLoop, calls=%fused_computation | loop fusion | flops 1572864 | bytes 1595648 | tf_op jit(solution)/shard_map/sin | solution.py:35
  57.0 2.0 collective-permute-done.4.side_ref
  59.0 0.0 copy-done.10
  59.0 0.0 copy-done.11
  59.0 0.8 norm.1.own_ref
  59.8 4.7 %collective-permute-start.5 = (bf16[4,192,512]{2,1,0:T(8,128)(2,1)S(1)}, bf16[4,192,512]{2,1,0:T(8,128)(2,1)}, u32[]{:S(2)}, u32[]{:S(2)}) collective-permute-start(bf16[4,192,512]{2,1,0:T(8,128)(2,1)S(1)} %norm.1.own_ref), channel_id=1, source_target_pairs={{0,32},{32,0},{1,33},{33,1},{2,34},{34,2},{3,35},{35,3},{4,36},{36... | collective-permute-start | bytes 2359304 | tf_op jit(solution)/shard_map/ppermute | solution.py:215
  64.5 0.1 pad_add_fusion.src_ref
  64.6 1.9 collective-permute-done.5.oth_ref
  66.5 0.0 copy-done.1
  66.5 0.0 copy-done.3
  66.5 1.1 copy-done.6
  67.6 2.9 %qkv.1 = (bf16[4,384,128]{2,1,0:T(8,128)(2,1)}, bf16[2,208,256]{2,1,0:T(8,128)(2,1)S(1)}, bf16[4,2,208,256]{3,2,1,0:T(8,128)(2,1)S(1)}) custom-call(s32[4]{0:T(128)S(1)} %pad_add_fusion.src_ref, s32[1]{0:T(128)} %bitcast.5.core_ref, bf16[4,192,512]{2,1,0:T(8,128)(2,1)S(1)} %norm.1.own_ref, bf16[4,192,512]{2,1,0:T(8,128)(2,1)} %collective-permute-done.5.oth_ref, ...), custom_call_target="tpu_custom_call" | custom-call | tf_op jit(solution)/shard_map/qkv/pallas_call | solution.py:216
  70.4 16.4 %all_to_all.30.kv_ref = bf16[4,2,208,256]{3,2,1,0:T(8,128)(2,1)S(1)} all-to-all(bf16[4,2,208,256]{3,2,1,0:T(8,128)(2,1)S(1)} %get-tuple-element.25), channel_id=1, replica_groups=mesh['y'=4,'zh'=2,'core'=2,'row'=4,'c2'=2,'c1'=2,'c0'=2] {'y'}, dimensions={0} | all-to-all | bytes 1703936 | tf_op jit(solution)/shard_map/all_to_all | solution.py:230
  86.8 4.4 %all-to-all-start.1 = ((bf16[4,384,128]{2,1,0:T(8,128)(2,1)}), bf16[4,384,128]{2,1,0:T(8,128)(2,1)S(1)}, u32[]{:S(2)}, u32[]{:S(2)}) async-start(bf16[4,384,128]{2,1,0:T(8,128)(2,1)} %get-tuple-element.23), calls=%async_computation.1 | async-start | bytes 786432 | tf_op jit(solution)/shard_map/all_to_all | solution.py:229
  91.2 8.6 %collective-permute-start.6 = (bf16[2,208,256]{2,1,0:T(8,128)(2,1)S(1)}, bf16[2,208,256]{2,1,0:T(8,128)(2,1)S(1)}, u32[]{:S(2)}, u32[]{:S(2)}) collective-permute-start(bf16[2,208,256]{2,1,0:T(8,128)(2,1)S(1)} %get-tuple-element.24), channel_id=1, source_target_pairs={{0,64},{1,65},{2,66},{3,67},{4,68},{5,69},{6,70},{7,71},{64,0},{65... | collective-permute-start | bytes 638984 | tf_op jit(solution)/shard_map/ppermute | solution.py:228
  99.8 7.0 %collective-permute-done.6 = bf16[2,208,256]{2,1,0:T(8,128)(2,1)S(1)} collective-permute-done((bf16[2,208,256]{2,1,0:T(8,128)(2,1)S(1)}, bf16[2,208,256]{2,1,0:T(8,128)(2,1)S(1)}, u32[]{:S(2)}, u32[]{:S(2)}) %collective-permute-start.6) | collective-permute-done | bytes 213024 | tf_op jit(solution)/shard_map/ppermute | solution.py:228
  106.8 0.0 all-to-all-done.1
  106.8 1.0 broadcast_in_dim.94
  107.8 3.5 %all-to-all-start.3 = ((bf16[4,2,208,256]{3,2,1,0:T(8,128)(2,1)}), bf16[4,2,208,256]{3,2,1,0:T(8,128)(2,1)S(1)}, u32[]{:S(2)}, u32[]{:S(2)}) async-start(bf16[4,2,208,256]{3,2,1,0:T(8,128)(2,1)} %broadcast_in_dim.94), calls=%async_computation.3 | async-start | bytes 1703936 | tf_op jit(solution)/shard_map/all_to_all | solution.py:40
  111.3 6.0 %near.1 = (f32[128,1536]{1,0:T(8,128)S(1)}, f32[8,1536]{1,0:T(8,128)S(1)}) custom-call(bf16[1536,128]{1,0:T(8,128)(2,1)S(1)} %bitcast.15, bf16[4,2,208,256]{3,2,1,0:T(8,128)(2,1)S(1)} %all_to_all.30.kv_ref), custom_call_target="tpu_custom_call" | custom-call | tf_op jit(solution)/shard_map/near/pallas_call | solution.py:237
  117.3 0.0 copy-start.8
  117.3 0.9 copy-done.8
  118.2 2.9 %all-to-all-done.3.kv_ref = bf16[4,2,208,256]{3,2,1,0:T(8,128)(2,1)S(1)} async-done(((bf16[4,2,208,256]{3,2,1,0:T(8,128)(2,1)}), bf16[4,2,208,256]{3,2,1,0:T(8,128)(2,1)S(1)}, u32[]{:S(2)}, u32[]{:S(2)}) %all-to-all-start.3) | async-done | bytes 852000 | tf_op jit(solution)/shard_map/all_to_all | solution.py:40
  121.1 1.1 copy-done.9
  122.3 7.0 %far.1 = bf16[8,208,128]{2,1,0:T(8,128)(2,1)} custom-call(bf16[1536,128]{1,0:T(8,128)(2,1)S(1)} %bitcast.16, bf16[4,2,208,256]{3,2,1,0:T(8,128)(2,1)S(1)} %all-to-all-done.3.kv_ref, f32[128,1536]{1,0:T(8,128)S(1)} %copy-done.9, f32[8,1536]{1,0:T(8,128)S(1)} %get-tuple-element.28.stat_ref), custom_call_target="tpu_custom_call" | custom-call | tf_op jit(solution)/shard_map/far/pallas_call | solution.py:250
  129.2 8.7 %all-to-all-start.4 = ((bf16[8,208,128]{2,1,0:T(8,128)(2,1)}), bf16[8,208,128]{2,1,0:T(8,128)(2,1)S(1)}, u32[]{:S(2)}, u32[]{:S(2)}) async-start(bf16[8,208,128]{2,1,0:T(8,128)(2,1)} %far.1), calls=%async_computation.4 | async-start | bytes 851968 | tf_op jit(solution)/shard_map/all_to_all | solution.py:263
  137.9 8.0 %all-to-all-done.4 = bf16[8,208,128]{2,1,0:T(8,128)(2,1)S(1)} async-done(((bf16[8,208,128]{2,1,0:T(8,128)(2,1)}), bf16[8,208,128]{2,1,0:T(8,128)(2,1)S(1)}, u32[]{:S(2)}, u32[]{:S(2)}) %all-to-all-start.4) | async-done | bytes 426016 | tf_op jit(solution)/shard_map/all_to_all | solution.py:263
  146.0 0.1 dynamic-slice_reduce_fusion
  146.1 0.1 fusion.16
  146.2 0.1 broadcast_divide_fusion
  146.3 0.3 multiply_reduce_fusion
  146.7 45.8 %all_to_all.31.near_ref = bf16[4,192,256]{2,1,0:T(8,128)(2,1)S(1)} all-to-all(bf16[4,192,256]{2,1,0:T(8,128)(2,1)S(1)} %broadcast_in_dim.95), channel_id=1, replica_groups=mesh['y'=4,'zh'=2,'core'=2,'row'=4,'c2'=2,'c1'=2,'c0'=2] {'c2','c1'}, dimensions={0} | all-to-all | bytes 786432 | tf_op jit(solution)/shard_map/all_to_all | solution.py:40
  192.5 1.9 collective-permute-start.7
  194.4 10.1 %collective-permute-done.7.side_ref = bf16[4,192,256]{2,1,0:T(8,128)(2,1)S(1)} collective-permute-done((bf16[4,192,256]{2,1,0:T(8,128)(2,1)S(1)}, bf16[4,192,256]{2,1,0:T(8,128)(2,1)S(1)}, u32[]{:S(2)}, u32[]{:S(2)}) %collective-permute-start.7) | collective-permute-done | bytes 393248 | tf_op jit(solution)/shard_map/ppermute | solution.py:271
  204.6 0.0 copy-done.2
  204.6 0.0 copy-done.4
  204.6 0.0 copy-done.7
  204.6 1.6 out.1
  (22 shorter events, 0.2 us)
Async XLA Ops:
  0.0 13.6 %copy-start = (bf16[512,256]{1,0:T(8,128)(2,1)S(1)}, bf16[512,256]{1,0:T(8,128)(2,1)}, u32[]{:S(2)}) copy-start(bf16[512,256]{1,0:T(8,128)(2,1)} %param.12) | copy-start | bytes 786436
  0.0 13.6 %copy-start.14 = (bf16[512,256]{1,0:T(8,128)(2,1)S(1)}, bf16[512,256]{1,0:T(8,128)(2,1)}, u32[]{:S(2)}) copy-start(bf16[512,256]{1,0:T(8,128)(2,1)} %param.13) | copy-start | bytes 786436
  0.0 13.6 %copy-start.13 = (bf16[512,256]{1,0:T(8,128)(2,1)S(1)}, bf16[512,256]{1,0:T(8,128)(2,1)}, u32[]{:S(2)}) copy-start(bf16[512,256]{1,0:T(8,128)(2,1)} %param.14) | copy-start | bytes 786436
  0.0 13.7 %copy-start.12 = (bf16[512,256]{1,0:T(8,128)(2,1)S(1)}, bf16[512,256]{1,0:T(8,128)(2,1)}, u32[]{:S(2)}) copy-start(bf16[512,256]{1,0:T(8,128)(2,1)} %param.15) | copy-start | bytes 786436
  1.8 22.0 %copy-start.15 = (s32[192]{0:T(256)S(1)}, s32[192]{0:T(256)}, u32[]{:S(2)}) copy-start(s32[192]{0:T(256)} %param.9) | copy-start | bytes 2308
  1.8 46.3 %all-to-all-start = ((bf16[4,192,256]{2,1,0:T(8,128)(2,1)}), bf16[4,192,256]{2,1,0:T(8,128)(2,1)S(1)}, u32[]{:S(2)}, u32[]{:S(2)}) async-start(bf16[4,192,256]{2,1,0:T(8,128)(2,1)} %broadcast_in_dim.85), calls=%async_computation | async-start | bytes 786432 | tf_op jit(solution)/shard_map/all_to_all | solution.py:40
  13.7 45.3 %copy-start.10 = (f32[2048]{0:T(1024)S(1)}, f32[2048]{0:T(1024)}, u32[]{:S(2)}) copy-start(f32[2048]{0:T(1024)} %param.10) | copy-start | bytes 24580
  13.7 45.3 %copy-start.11 = (f32[2048]{0:T(1024)S(1)}, f32[2048]{0:T(1024)}, u32[]{:S(2)}) copy-start(f32[2048]{0:T(1024)} %param.11) | copy-start | bytes 24580
  13.8 18.4 %collective-permute-start = (bf16[512,640]{1,0:T(8,128)(2,1)S(1)}, bf16[512,640]{1,0:T(8,128)(2,1)S(1)}, u32[]{:S(2)}, u32[]{:S(2)}) collective-permute-start(bf16[512,640]{1,0:T(8,128)(2,1)S(1)} %pad_maximum_fusion.w0_ref), channel_id=1, source_target_pairs={{0,8},{8,16},{16,24},{24,0},{1,9},{9,17},{17,25},{25,1},{2,10},{10... | collective-permute-start | bytes 1966088 | tf_op jit(solution)/shard_map/ppermute | solution.py:195
  16.9 16.9 %collective-permute-start.1 = (bf16[512,640]{1,0:T(8,128)(2,1)S(1)}, bf16[512,640]{1,0:T(8,128)(2,1)S(1)}, u32[]{:S(2)}, u32[]{:S(2)}) collective-permute-start(bf16[512,640]{1,0:T(8,128)(2,1)S(1)} %pad_maximum_fusion.w0_ref), channel_id=1, source_target_pairs={{0,24},{8,0},{16,8},{24,16},{1,25},{9,1},{17,9},{25,17},{2,26},{10... | collective-permute-start | bytes 1966088 | tf_op jit(solution)/shard_map/ppermute | solution.py:195
  20.3 27.0 %collective-permute-start.2 = (bf16[512,640]{1,0:T(8,128)(2,1)S(1)}, bf16[512,640]{1,0:T(8,128)(2,1)S(1)}, u32[]{:S(2)}, u32[]{:S(2)}) collective-permute-start(bf16[512,640]{1,0:T(8,128)(2,1)S(1)} %pad_maximum_fusion.w0_ref), channel_id=1, source_target_pairs={{0,16},{8,24},{16,0},{24,8},{1,17},{9,25},{17,1},{25,9},{2,18},{10... | collective-permute-start | bytes 1966088 | tf_op jit(solution)/shard_map/ppermute | solution.py:195
  25.0 4.5 %collective-permute-start.3 = (f32[16,256]{1,0:T(8,128)S(1)}, f32[16,256]{1,0:T(8,128)S(1)}, u32[]{:S(2)}, u32[]{:S(2)}) collective-permute-start(f32[16,256]{1,0:T(8,128)S(1)} %broadcast_in_dim.86), channel_id=1, source_target_pairs={{0,32},{32,0},{1,33},{33,1},{2,34},{34,2},{3,35},{35,3},{4,36},{36... | collective-permute-start | bytes 49160 | tf_op jit(solution)/shard_map/ppermute | solution.py:201
  32.3 34.2 %copy-start.1 = (bf16[512,640]{1,0:T(8,128)(2,1)}, bf16[512,640]{1,0:T(8,128)(2,1)S(1)}, u32[]{:S(2)}) copy-start(bf16[512,640]{1,0:T(8,128)(2,1)S(1)} %collective-permute-done.w1_ref) | copy-start | bytes 1966084
  33.9 32.6 %copy-start.3 = (bf16[512,640]{1,0:T(8,128)(2,1)}, bf16[512,640]{1,0:T(8,128)(2,1)S(1)}, u32[]{:S(2)}) copy-start(bf16[512,640]{1,0:T(8,128)(2,1)S(1)} %collective-permute-done.1.w2_ref) | copy-start | bytes 1966084
  47.3 0.8 copy-start.5
  48.1 10.8 %collective-permute-start.4 = (bf16[4,192,256]{2,1,0:T(8,128)(2,1)S(1)}, bf16[4,192,256]{2,1,0:T(8,128)(2,1)S(1)}, u32[]{:S(2)}, u32[]{:S(2)}) collective-permute-start(bf16[4,192,256]{2,1,0:T(8,128)(2,1)S(1)} %all-to-all-done.near_ref), channel_id=1, source_target_pairs={{0,1},{1,0},{2,3},{3,2},{4,5},{5,4},{6,7},{7,6},{8,9},{9,8},{10,11... | collective-permute-start | bytes 1179656 | tf_op jit(solution)/shard_map/ppermute | solution.py:206
  59.8 6.7 %collective-permute-start.5 = (bf16[4,192,512]{2,1,0:T(8,128)(2,1)S(1)}, bf16[4,192,512]{2,1,0:T(8,128)(2,1)}, u32[]{:S(2)}, u32[]{:S(2)}) collective-permute-start(bf16[4,192,512]{2,1,0:T(8,128)(2,1)S(1)} %norm.1.own_ref), channel_id=1, source_target_pairs={{0,32},{32,0},{1,33},{33,1},{2,34},{34,2},{3,35},{35,3},{4,36},{36... | collective-permute-start | bytes 2359304 | tf_op jit(solution)/shard_map/ppermute | solution.py:215
  66.5 1.1 copy-start.6
  86.8 20.0 %all-to-all-start.1 = ((bf16[4,384,128]{2,1,0:T(8,128)(2,1)}), bf16[4,384,128]{2,1,0:T(8,128)(2,1)S(1)}, u32[]{:S(2)}, u32[]{:S(2)}) async-start(bf16[4,384,128]{2,1,0:T(8,128)(2,1)} %get-tuple-element.23), calls=%async_computation.1 | async-start | bytes 786432 | tf_op jit(solution)/shard_map/all_to_all | solution.py:229
  91.2 15.6 %collective-permute-start.6 = (bf16[2,208,256]{2,1,0:T(8,128)(2,1)S(1)}, bf16[2,208,256]{2,1,0:T(8,128)(2,1)S(1)}, u32[]{:S(2)}, u32[]{:S(2)}) collective-permute-start(bf16[2,208,256]{2,1,0:T(8,128)(2,1)S(1)} %get-tuple-element.24), channel_id=1, source_target_pairs={{0,64},{1,65},{2,66},{3,67},{4,68},{5,69},{6,70},{7,71},{64,0},{65... | collective-permute-start | bytes 638984 | tf_op jit(solution)/shard_map/ppermute | solution.py:228
  107.8 13.3 %all-to-all-start.3 = ((bf16[4,2,208,256]{3,2,1,0:T(8,128)(2,1)}), bf16[4,2,208,256]{3,2,1,0:T(8,128)(2,1)S(1)}, u32[]{:S(2)}, u32[]{:S(2)}) async-start(bf16[4,2,208,256]{3,2,1,0:T(8,128)(2,1)} %broadcast_in_dim.94), calls=%async_computation.3 | async-start | bytes 1703936 | tf_op jit(solution)/shard_map/all_to_all | solution.py:40
  117.3 0.9 copy-start.8
  121.1 1.1 copy-start.9
  129.2 75.3 %copy-start.2 = (bf16[512,640]{1,0:T(8,128)(2,1)S(1)}, bf16[512,640]{1,0:T(8,128)(2,1)}, u32[]{:S(2)}) copy-start(bf16[512,640]{1,0:T(8,128)(2,1)} %copy-done.1) | copy-start | bytes 1966084
  129.2 75.3 %copy-start.4 = (bf16[512,640]{1,0:T(8,128)(2,1)S(1)}, bf16[512,640]{1,0:T(8,128)(2,1)}, u32[]{:S(2)}) copy-start(bf16[512,640]{1,0:T(8,128)(2,1)} %copy-done.3) | copy-start | bytes 1966084
  129.2 75.3 %copy-start.7 = (bf16[512,640]{1,0:T(8,128)(2,1)S(1)}, bf16[512,640]{1,0:T(8,128)(2,1)}, u32[]{:S(2)}) copy-start(bf16[512,640]{1,0:T(8,128)(2,1)} %copy-done.5) | copy-start | bytes 1966084
  129.2 16.7 %all-to-all-start.4 = ((bf16[8,208,128]{2,1,0:T(8,128)(2,1)}), bf16[8,208,128]{2,1,0:T(8,128)(2,1)S(1)}, u32[]{:S(2)}, u32[]{:S(2)}) async-start(bf16[8,208,128]{2,1,0:T(8,128)(2,1)} %far.1), calls=%async_computation.4 | async-start | bytes 851968 | tf_op jit(solution)/shard_map/all_to_all | solution.py:263
  192.5 12.1 %collective-permute-start.7 = (bf16[4,192,256]{2,1,0:T(8,128)(2,1)S(1)}, bf16[4,192,256]{2,1,0:T(8,128)(2,1)S(1)}, u32[]{:S(2)}, u32[]{:S(2)}) collective-permute-start(bf16[4,192,256]{2,1,0:T(8,128)(2,1)S(1)} %all_to_all.31.near_ref), channel_id=1, source_target_pairs={{0,1},{1,0},{2,3},{3,2},{4,5},{5,4},{6,7},{7,6},{8,9},{9,8},{10,11... | collective-permute-start | bytes 1179656 | tf_op jit(solution)/shard_map/ppermute | solution.py:271
where the time goes:
time: 207 us; the launch traced here: 206 us
  blocking collectives  62.3 us (30%)
  starting transfers between devices  60.8 us (29%)
  waiting for transfers between devices  49.7 us (24%)
  Pallas kernels  18.2 us (9%)
  local copies, waits for them, and re-layouts  8.14 us (4%)
  other arithmetic  6.77 us (3%)
    all_to_all x1, blocking collectives, spread(): return lax.all_to_all(copies, axes, 0, 0)  45.8 us
    ppermute x3, waiting for transfers between devices, sublayer(): weights += [lax.ppermute(w_own, 'row', ring(4, s)) for s in SHIFTS[1:]]  17.1 us
    all_to_all x1, blocking collectives, sublayer(): near_kv = lax.all_to_all(near_kv, 'y', 0, 0)  16.4 us
    all_to_all x2, starting transfers between devices, spread(): return lax.all_to_all(copies, axes, 0, 0)  15.3 us
    ppermute x2, waiting for transfers between devices, sublayer(): side = lax.ppermute(near, 'c0', ring(2, 1))  12.1 us
    ppermute x3, starting transfers between devices, sublayer(): weights += [lax.ppermute(w_own, 'row', ring(4, s)) for s in SHIFTS[1:]]  9.93 us
    all_to_all x1, starting transfers between devices, sublayer(): lax.all_to_all(part, ('row', 'core'), 0, 0).reshape(4, 2, ROWS + 16, 128)  8.7 us
    ppermute x1, starting transfers between devices, sublayer(): far_kv = lax.ppermute(kv, ('zh', 'c2', 'c1', 'c0'), ring(16, 8))  8.64 us
  transfers between devices with their start and end apart: 12, of which 10 were waited for; matrix products, arithmetic and copies ran while one was open for 4% of the time, Pallas kernels for 3%

commit v1 on v0

--- a/solution.py
+++ b/solution.py
@@ -72,7 +72,7 @@
     for c, n_ref in enumerate((own_ref, oth_ref)):
         acc = jnp.zeros((ROWS, 384), F32)
         for s, w_ref in enumerate((w0_ref, w1_ref, w2_ref, w3_ref)):
-            acc = acc + jnp.dot(n_ref[src_ref[s]], w_ref[:, :384], preferred_element_type=F32)
+            acc = acc + jnp.dot(n_ref[src_ref[s]], w_ref[...], preferred_element_type=F32)
         at = pl.multiple_of((core_ref[0] ^ c) * ROWS, ROWS)
         query = (acc[:, :128] * (1.0 / math.sqrt(HEAD_DIM))).astype(BF16)
         pair = acc[:, 128:384].astype(BF16)
@@ -166,13 +166,15 @@
             out_ref[2 * x + c, ROWS : ROWS + 16, :] = stats
 
 
-def out_kernel(src_ref, par_ref, near_ref, side_ref, w0_ref, w1_ref, w2_ref, w3_ref, out_ref):
+def out_kernel(src_ref, half_ref, m_ref, w0_ref, w1_ref, w2_ref, w3_ref, out_ref):
     acc = jnp.zeros(out_ref.shape, F32)
     for s, w_ref in enumerate((w0_ref, w1_ref, w2_ref, w3_ref)):
-        for flip, m_ref in enumerate((near_ref, side_ref)):
-            at = pl.multiple_of((par_ref[0] ^ flip) * 256, 256)
+        for step in range(2):
+            at = src_ref[s] + step
             acc = acc + jnp.dot(
-                m_ref[src_ref[s]], w_ref[pl.ds(at, 256), 384:640], preferred_element_type=F32
+                m_ref[at % 4, half_ref[0] ^ (at // 4)],
+                w_ref[step * 256 : (step + 1) * 256, :],
+                preferred_element_type=F32,
             )
     out_ref[...] = acc
 
@@ -187,22 +189,25 @@
     row = lax.axis_index("row")
     lane = core * HEAD_DIM
     w_own = jnp.concatenate(
-        [lax.dynamic_slice_in_dim(w, lane, HEAD_DIM, 1) for w in (w_query, w_key, w_value)]
-        + [w_output],
+        [lax.dynamic_slice_in_dim(w, lane, HEAD_DIM, 1) for w in (w_query, w_key, w_value)],
         axis=1,
     )
     weights = [w_own]
     weights += [lax.ppermute(w_own, "row", ring(4, s)) for s in SHIFTS[1:]]
+    outward = [w_output]
+    outward += [lax.ppermute(w_output, "row", ring(4, s)) for s in SHIFTS[1:]]
     source = jnp.stack([(row - s) % 4 for s in SHIFTS]).astype(jnp.int32)
+    chunks = jnp.stack([(row - s) % 4 * 2 for s in SHIFTS]).astype(jnp.int32)
     core = core.astype(jnp.int32)[None]
     parity = lax.axis_index("c0").astype(jnp.int32)[None]
+    half = lax.axis_index("c2").astype(jnp.int32)[None]
 
     live = jnp.full((16, 256), jnp.sum((visible >= 0).astype(F32)), F32)
     counts = jnp.stack([live, lax.ppermute(live, "core", ring(2, 1))])
 
     pos = embed(visible, 2048)
     near = spread(patches, ("c2", "c1"), 4)
-    near, weights, counts = lax.optimization_barrier((near, weights, counts))
+    near, counts = lax.optimization_barrier((near, counts))
     side = lax.ppermute(near, "c0", ring(2, 1))
     own = pl.pallas_call(
         norm_kernel,
@@ -267,16 +272,17 @@
     share = share / jnp.sum(share, axis=0, keepdims=True)
     mixed = jnp.sum(part[:, :, :ROWS, :].astype(F32) * share[..., None], axis=0)
     mixed = jnp.concatenate([mixed[0], mixed[1]], axis=1).astype(BF16)
-    near = spread(mixed, ("c2", "c1"), 4)
-    side = lax.ppermute(near, "c0", ring(2, 1))
+    swapped = lax.ppermute(mixed, "c2", ring(2, 1))
+    mixed = jnp.stack([mixed, swapped])
+    mixed = spread(mixed, ("c1", "c0"), 4)
     return pl.pallas_call(
         out_kernel,
         out_shape=jax.ShapeDtypeStruct((ROWS, 256), F32),
-        in_specs=[SMEM] * 2 + [VMEM] * 6,
+        in_specs=[SMEM] * 2 + [VMEM] * 5,
         out_specs=VMEM,
         compiler_params=PARAMS,
         name="out",
-    )(source, parity, near, side, *weights)
+    )(chunks, half, mixed, *outward)
 
 
 def solution(mesh):

time: 207 us -> 201 us (0.971)
  blocking collectives: 62.3 us -> 15.7 us
  starting transfers between devices: 60.8 us -> 91.4 us
  waiting for transfers between devices: 49.7 us -> 62.1 us
  local copies, waits for them, and re-layouts: 8.14 us -> 4.95 us
    all_to_all x1 -> x0, blocking collectives: 45.8 us -> none  [spread(): return lax.all_to_all(copies, axes, 0, 0)]
    all_to_all x2 -> x3, waiting for transfers between devices: 2.94 us -> 19 us  [spread(): return lax.all_to_all(copies, axes, 0, 0)]
    ppermute x0 -> x4, waiting for transfers between devices: none -> 14.9 us  [the longest x3 7.55 us: sublayer(): outward += [lax.ppermute(w_output, 'row', ring(4, s)) for s in SHIFTS[1:]]]
    all_to_all x2 -> x3, starting transfers between devices: 15.3 us -> 27.2 us  [spread(): return lax.all_to_all(copies, axes, 0, 0)]
    ppermute x0 -> x4, starting transfers between devices: none -> 10.5 us  [the longest x3 8.4 us: sublayer(): outward += [lax.ppermute(w_output, 'row', ring(4, s)) for s in SHIFTS[1:]]]
    ppermute x2 -> x1, waiting for transfers between devices: 12.1 us -> 2 us  [sublayer(): side = lax.ppermute(near, 'c0', ring(2, 1))]
    all_to_all x1, starting transfers between devices: 8.7 us -> 16.2 us  [sublayer(): lax.all_to_all(part, ('row', 'core'), 0, 0).reshape(4, 2, ROWS + 16, 128)]
    unnamed x32 -> x14, local copies, waits for them, and re-layouts: 4.02 us -> 0.03 us
  transfers between devices with their start and end apart: 12 -> 16, of which waited for: 10 -> 14; matrix products, arithmetic and copies ran while one was open for 4% -> 4% of each run, Pallas kernels for 3% -> 3%
where the time goes in v1:
time: 201 us; the launch traced here: 200 us
  starting transfers between devices  91.4 us (45%)
  waiting for transfers between devices  62.1 us (31%)
  Pallas kernels  17.6 us (9%)
  blocking collectives  15.7 us (8%)
  other arithmetic  8.21 us (4%)
  local copies, waits for them, and re-layouts  4.95 us (2%)
    all_to_all x3, starting transfers between devices, spread(): return lax.all_to_all(copies, axes, 0, 0)  27.2 us
    all_to_all x3, waiting for transfers between devices, spread(): return lax.all_to_all(copies, axes, 0, 0)  19 us
    all_to_all x1, starting transfers between devices, sublayer(): lax.all_to_all(part, ('row', 'core'), 0, 0).reshape(4, 2, ROWS + 16, 128)  16.2 us
    all_to_all x1, blocking collectives, sublayer(): near_kv = lax.all_to_all(near_kv, 'y', 0, 0)  15.7 us
    ppermute x3, waiting for transfers between devices, sublayer(): weights += [lax.ppermute(w_own, 'row', ring(4, s)) for s in SHIFTS[1:]]  13.1 us
    ppermute x1, starting transfers between devices, sublayer(): far_kv = lax.ppermute(kv, ('zh', 'c2', 'c1', 'c0'), ring(16, 8))  10.7 us
    ppermute x3, starting transfers between devices, sublayer(): weights += [lax.ppermute(w_own, 'row', ring(4, s)) for s in SHIFTS[1:]]  9.93 us
    ppermute x3, starting transfers between devices, sublayer(): outward += [lax.ppermute(w_output, 'row', ring(4, s)) for s in SHIFTS[1:]]  8.4 us
  transfers between devices with their start and end apart: 16, of which 14 were waited for; matrix products, arithmetic and copies ran while one was open for 4% of the time, Pallas kernels for 3%

profile of v1, /device:TPU:1, one launch (start us, length us, event | category | flops | bytes accessed | tf_op | source)
XLA Modules:
  0.0 200.3 jit_solution(17354016391937228346)
XLA Ops:
  0.0 0.0 copy-start
  0.0 0.0 copy-start.2
  0.0 0.0 copy-start.3
  0.0 1.7 broadcast_in_dim.89
  1.7 11.7 %all-to-all-start = ((bf16[4,192,256]{2,1,0:T(8,128)(2,1)}), bf16[4,192,256]{2,1,0:T(8,128)(2,1)S(1)}, u32[]{:S(2)}, u32[]{:S(2)}) async-start(bf16[4,192,256]{2,1,0:T(8,128)(2,1)} %broadcast_in_dim.89), calls=%async_computation | async-start | bytes 786432 | tf_op jit(solution)/shard_map/all_to_all | solution.py:40
  13.4 1.3 fusion.17
  14.7 0.6 broadcast_in_dim.90
  15.3 2.9 %collective-permute-start = (f32[16,256]{1,0:T(8,128)S(1)}, f32[16,256]{1,0:T(8,128)S(1)}, u32[]{:S(2)}, u32[]{:S(2)}) collective-permute-start(f32[16,256]{1,0:T(8,128)S(1)} %broadcast_in_dim.90), channel_id=1, source_target_pairs={{0,32},{32,0},{1,33},{33,1},{2,34},{34,2},{3,35},{35,3},{4,36},{36... | collective-permute-start | bytes 49160 | tf_op jit(solution)/shard_map/ppermute | solution.py:206
  18.2 0.7 fusion.18
  19.0 0.1 collective-permute-done
  19.0 0.6 stack.54.cnt_ref
  19.7 12.7 %all-to-all-done.near_ref = bf16[4,192,256]{2,1,0:T(8,128)(2,1)S(1)} async-done(((bf16[4,192,256]{2,1,0:T(8,128)(2,1)}), bf16[4,192,256]{2,1,0:T(8,128)(2,1)S(1)}, u32[]{:S(2)}, u32[]{:S(2)}) %all-to-all-start) | async-done | bytes 393248 | tf_op jit(solution)/shard_map/all_to_all | solution.py:40
  32.3 5.7 %collective-permute-start.1 = (bf16[4,192,256]{2,1,0:T(8,128)(2,1)S(1)}, bf16[4,192,256]{2,1,0:T(8,128)(2,1)S(1)}, u32[]{:S(2)}, u32[]{:S(2)}) collective-permute-start(bf16[4,192,256]{2,1,0:T(8,128)(2,1)S(1)} %all-to-all-done.near_ref), channel_id=1, source_target_pairs={{0,1},{1,0},{2,3},{3,2},{4,5},{5,4},{6,7},{7,6},{8,9},{9,8},{10,11... | collective-permute-start | bytes 1179656 | tf_op jit(solution)/shard_map/ppermute | solution.py:211
  38.0 5.3 %add_sine_fusion.pos_ref = f32[192,2048]{1,0:T(8,128)S(1)} fusion(f32[2048]{0:T(1024)S(1)} %get-tuple-element.27, f32[2048]{0:T(1024)S(1)} %get-tuple-element.26, f32[192]{0:T(256)S(1)} %get-tuple-element.25, f32[192]{0:T(256)S(1)} %get-tuple-element.24, f32[192]{0:T(256)S(1)} %get-tuple-element.23, pred[2048]{0:T(1024)(128)(4,1)S(1)} %get-tuple-element.28, ...), kind=kLoop, calls=%fused_computation | loop fusion | flops 1572864 | bytes 1595648 | tf_op jit(solution)/shard_map/sin | solution.py:35
  43.4 2.0 %collective-permute-done.1.side_ref = bf16[4,192,256]{2,1,0:T(8,128)(2,1)S(1)} collective-permute-done((bf16[4,192,256]{2,1,0:T(8,128)(2,1)S(1)}, bf16[4,192,256]{2,1,0:T(8,128)(2,1)S(1)}, u32[]{:S(2)}, u32[]{:S(2)}) %collective-permute-start.1) | collective-permute-done | bytes 393248 | tf_op jit(solution)/shard_map/ppermute | solution.py:211
  45.4 0.0 copy-done.2
  45.4 0.0 copy-done.3
  45.4 0.8 norm.1.own_ref
  46.2 4.6 %collective-permute-start.2 = (bf16[4,192,512]{2,1,0:T(8,128)(2,1)S(1)}, bf16[4,192,512]{2,1,0:T(8,128)(2,1)S(1)}, u32[]{:S(2)}, u32[]{:S(2)}) collective-permute-start(bf16[4,192,512]{2,1,0:T(8,128)(2,1)S(1)} %norm.1.own_ref), channel_id=1, source_target_pairs={{0,32},{32,0},{1,33},{33,1},{2,34},{34,2},{3,35},{35,3},{4,36},{36... | collective-permute-start | bytes 2359304 | tf_op jit(solution)/shard_map/ppermute | solution.py:220
  50.8 0.0 copy-done
  50.9 0.0 copy-done.5
  50.9 0.0 copy-done.6
  50.9 0.1 pad_maximum_fusion.w0_ref
  51.0 3.1 %collective-permute-start.3 = (bf16[512,384]{1,0:T(8,128)(2,1)S(1)}, bf16[512,384]{1,0:T(8,128)(2,1)S(1)}, u32[]{:S(2)}, u32[]{:S(2)}) collective-permute-start(bf16[512,384]{1,0:T(8,128)(2,1)S(1)} %pad_maximum_fusion.w0_ref), channel_id=1, source_target_pairs={{0,8},{8,16},{16,24},{24,0},{1,9},{9,17},{17,25},{25,1},{2,10},{10... | collective-permute-start | bytes 1179656 | tf_op jit(solution)/shard_map/ppermute | solution.py:196
  54.1 3.4 %collective-permute-start.4 = (bf16[512,384]{1,0:T(8,128)(2,1)S(1)}, bf16[512,384]{1,0:T(8,128)(2,1)S(1)}, u32[]{:S(2)}, u32[]{:S(2)}) collective-permute-start(bf16[512,384]{1,0:T(8,128)(2,1)S(1)} %pad_maximum_fusion.w0_ref), channel_id=1, source_target_pairs={{0,24},{8,0},{16,8},{24,16},{1,25},{9,1},{17,9},{25,17},{2,26},{10... | collective-permute-start | bytes 1179656 | tf_op jit(solution)/shard_map/ppermute | solution.py:196
  57.5 3.4 %collective-permute-start.5 = (bf16[512,384]{1,0:T(8,128)(2,1)S(1)}, bf16[512,384]{1,0:T(8,128)(2,1)S(1)}, u32[]{:S(2)}, u32[]{:S(2)}) collective-permute-start(bf16[512,384]{1,0:T(8,128)(2,1)S(1)} %pad_maximum_fusion.w0_ref), channel_id=1, source_target_pairs={{0,16},{8,24},{16,0},{24,8},{1,17},{9,25},{17,1},{25,9},{2,18},{10... | collective-permute-start | bytes 1179656 | tf_op jit(solution)/shard_map/ppermute | solution.py:196
  61.0 0.1 pad_add_fusion.1.src_ref
  61.1 3.7 %collective-permute-done.3.w1_ref = bf16[512,384]{1,0:T(8,128)(2,1)S(1)} collective-permute-done((bf16[512,384]{1,0:T(8,128)(2,1)S(1)}, bf16[512,384]{1,0:T(8,128)(2,1)S(1)}, u32[]{:S(2)}, u32[]{:S(2)}) %collective-permute-start.3) | collective-permute-done | bytes 393248 | tf_op jit(solution)/shard_map/ppermute | solution.py:196
  64.8 1.6 collective-permute-done.4.w2_ref
  66.4 7.8 %collective-permute-done.5.w3_ref = bf16[512,384]{1,0:T(8,128)(2,1)S(1)} collective-permute-done((bf16[512,384]{1,0:T(8,128)(2,1)S(1)}, bf16[512,384]{1,0:T(8,128)(2,1)S(1)}, u32[]{:S(2)}, u32[]{:S(2)}) %collective-permute-start.5) | collective-permute-done | bytes 393248 | tf_op jit(solution)/shard_map/ppermute | solution.py:196
  74.2 0.0 collective-permute-done.2.oth_ref
  74.2 2.3 %qkv.1 = (bf16[4,384,128]{2,1,0:T(8,128)(2,1)}, bf16[2,208,256]{2,1,0:T(8,128)(2,1)S(1)}, bf16[4,2,208,256]{3,2,1,0:T(8,128)(2,1)S(1)}) custom-call(s32[4]{0:T(128)S(1)} %pad_add_fusion.1.src_ref, s32[1]{0:T(128)} %bitcast.9.core_ref, bf16[4,192,512]{2,1,0:T(8,128)(2,1)S(1)} %norm.1.own_ref, bf16[4,192,512]{2,1,0:T(8,128)(2,1)S(1)} %collective-permute-done.2.oth_ref, ...), custom_call_target="tpu_custom_call" | custom-call | tf_op jit(solution)/shard_map/qkv/pallas_call | solution.py:221
  76.4 15.7 %all_to_all.30.kv_ref = bf16[4,2,208,256]{3,2,1,0:T(8,128)(2,1)S(1)} all-to-all(bf16[4,2,208,256]{3,2,1,0:T(8,128)(2,1)S(1)} %get-tuple-element.17), channel_id=1, replica_groups=mesh['y'=4,'zh'=2,'core'=2,'row'=4,'c2'=2,'c1'=2,'c0'=2] {'y'}, dimensions={0} | all-to-all | bytes 1703936 | tf_op jit(solution)/shard_map/all_to_all | solution.py:235
  92.1 0.0 copy-done.4
  92.1 3.8 %all-to-all-start.1 = ((bf16[4,384,128]{2,1,0:T(8,128)(2,1)}), bf16[4,384,128]{2,1,0:T(8,128)(2,1)S(1)}, u32[]{:S(2)}, u32[]{:S(2)}) async-start(bf16[4,384,128]{2,1,0:T(8,128)(2,1)} %get-tuple-element.15), calls=%async_computation.1 | async-start | bytes 786432 | tf_op jit(solution)/shard_map/all_to_all | solution.py:234
  95.9 10.7 %collective-permute-start.6 = (bf16[2,208,256]{2,1,0:T(8,128)(2,1)}, bf16[2,208,256]{2,1,0:T(8,128)(2,1)S(1)}, u32[]{:S(2)}, u32[]{:S(2)}) collective-permute-start(bf16[2,208,256]{2,1,0:T(8,128)(2,1)} %copy-done.4), channel_id=1, source_target_pairs={{0,64},{1,65},{2,66},{3,67},{4,68},{5,69},{6,70},{7,71},{64,0},{65... | collective-permute-start | bytes 638984 | tf_op jit(solution)/shard_map/ppermute | solution.py:233
  106.6 5.1 %collective-permute-done.6 = bf16[2,208,256]{2,1,0:T(8,128)(2,1)S(1)} collective-permute-done((bf16[2,208,256]{2,1,0:T(8,128)(2,1)}, bf16[2,208,256]{2,1,0:T(8,128)(2,1)S(1)}, u32[]{:S(2)}, u32[]{:S(2)}) %collective-permute-start.6) | collective-permute-done | bytes 213024 | tf_op jit(solution)/shard_map/ppermute | solution.py:233
  111.7 0.0 all-to-all-done.1
  111.7 1.0 broadcast_in_dim.98
  112.7 3.5 %all-to-all-start.3 = ((bf16[4,2,208,256]{3,2,1,0:T(8,128)(2,1)}), bf16[4,2,208,256]{3,2,1,0:T(8,128)(2,1)S(1)}, u32[]{:S(2)}, u32[]{:S(2)}) async-start(bf16[4,2,208,256]{3,2,1,0:T(8,128)(2,1)} %broadcast_in_dim.98), calls=%async_computation.3 | async-start | bytes 1703936 | tf_op jit(solution)/shard_map/all_to_all | solution.py:40
  116.2 6.0 %near.1 = (f32[128,1536]{1,0:T(8,128)S(1)}, f32[8,1536]{1,0:T(8,128)S(1)}) custom-call(bf16[1536,128]{1,0:T(8,128)(2,1)S(1)} %bitcast.19, bf16[4,2,208,256]{3,2,1,0:T(8,128)(2,1)S(1)} %all_to_all.30.kv_ref), custom_call_target="tpu_custom_call" | custom-call | tf_op jit(solution)/shard_map/near/pallas_call | solution.py:242
  122.1 2.7 %all-to-all-done.3.kv_ref = bf16[4,2,208,256]{3,2,1,0:T(8,128)(2,1)S(1)} async-done(((bf16[4,2,208,256]{3,2,1,0:T(8,128)(2,1)}), bf16[4,2,208,256]{3,2,1,0:T(8,128)(2,1)S(1)}, u32[]{:S(2)}, u32[]{:S(2)}) %all-to-all-start.3) | async-done | bytes 852000 | tf_op jit(solution)/shard_map/all_to_all | solution.py:40
  124.8 7.0 %far.1 = bf16[8,208,128]{2,1,0:T(8,128)(2,1)} custom-call(bf16[1536,128]{1,0:T(8,128)(2,1)S(1)} %bitcast.20, bf16[4,2,208,256]{3,2,1,0:T(8,128)(2,1)S(1)} %all-to-all-done.3.kv_ref, f32[128,1536]{1,0:T(8,128)S(1)} %get-tuple-element.19.part_ref, f32[8,1536]{1,0:T(8,128)S(1)} %get-tuple-element.20.stat_ref), custom_call_target="tpu_custom_call" | custom-call | tf_op jit(solution)/shard_map/far/pallas_call | solution.py:255
  131.8 16.2 %all-to-all-start.4 = ((bf16[8,208,128]{2,1,0:T(8,128)(2,1)}), bf16[8,208,128]{2,1,0:T(8,128)(2,1)S(1)}, u32[]{:S(2)}, u32[]{:S(2)}) async-start(bf16[8,208,128]{2,1,0:T(8,128)(2,1)} %far.1), calls=%async_computation.4 | async-start | bytes 851968 | tf_op jit(solution)/shard_map/all_to_all | solution.py:268
  148.0 8.0 %all-to-all-done.4 = bf16[8,208,128]{2,1,0:T(8,128)(2,1)S(1)} async-done(((bf16[8,208,128]{2,1,0:T(8,128)(2,1)}), bf16[8,208,128]{2,1,0:T(8,128)(2,1)S(1)}, u32[]{:S(2)}, u32[]{:S(2)}) %all-to-all-start.4) | async-done | bytes 426016 | tf_op jit(solution)/shard_map/all_to_all | solution.py:268
  156.1 0.1 dynamic-slice_reduce_fusion
  156.2 0.1 fusion.16
  156.3 0.1 broadcast_divide_fusion
  156.4 0.3 multiply_reduce_fusion
  156.7 0.0 copy-start.1
  156.7 2.1 %collective-permute-start.7 = (bf16[192,256]{1,0:T(8,128)(2,1)S(1)}, bf16[192,256]{1,0:T(8,128)(2,1)S(1)}, u32[]{:S(2)}, u32[]{:S(2)}) collective-permute-start(bf16[192,256]{1,0:T(8,128)(2,1)S(1)} %pad_maximum_fusion.2), channel_id=1, source_target_pairs={{0,4},{4,0},{1,5},{5,1},{2,6},{6,2},{3,7},{7,3},{8,12},{12,8},{9,1... | collective-permute-start | bytes 294920 | tf_op jit(solution)/shard_map/ppermute | solution.py:275
  158.8 7.3 %collective-permute-done.7 = bf16[192,256]{1,0:T(8,128)(2,1)S(1)} collective-permute-done((bf16[192,256]{1,0:T(8,128)(2,1)S(1)}, bf16[192,256]{1,0:T(8,128)(2,1)S(1)}, u32[]{:S(2)}, u32[]{:S(2)}) %collective-permute-start.7) | collective-permute-done | bytes 98336 | tf_op jit(solution)/shard_map/ppermute | solution.py:275
  166.1 0.9 broadcast_in_dim.99
  167.1 12.0 %all-to-all-start.5 = ((bf16[4,2,192,256]{3,2,1,0:T(8,128)(2,1)}), bf16[4,2,192,256]{3,2,1,0:T(8,128)(2,1)S(1)}, u32[]{:S(2)}, u32[]{:S(2)}) async-start(bf16[4,2,192,256]{3,2,1,0:T(8,128)(2,1)} %broadcast_in_dim.99), calls=%async_computation.5 | async-start | bytes 1572864 | tf_op jit(solution)/shard_map/all_to_all | solution.py:40
  179.0 0.0 copy-done.1
  179.0 2.2 %collective-permute-start.8 = (bf16[512,256]{1,0:T(8,128)(2,1)S(1)}, bf16[512,256]{1,0:T(8,128)(2,1)S(1)}, u32[]{:S(2)}, u32[]{:S(2)}) collective-permute-start(bf16[512,256]{1,0:T(8,128)(2,1)S(1)} %copy-done.1), channel_id=1, source_target_pairs={{0,8},{8,16},{16,24},{24,0},{1,9},{9,17},{17,25},{25,1},{2,10},{10... | collective-permute-start | bytes 786440 | tf_op jit(solution)/shard_map/ppermute | solution.py:198
  181.2 4.3 %collective-permute-start.9 = (bf16[512,256]{1,0:T(8,128)(2,1)S(1)}, bf16[512,256]{1,0:T(8,128)(2,1)S(1)}, u32[]{:S(2)}, u32[]{:S(2)}) collective-permute-start(bf16[512,256]{1,0:T(8,128)(2,1)S(1)} %copy-done.1), channel_id=1, source_target_pairs={{0,24},{8,0},{16,8},{24,16},{1,25},{9,1},{17,9},{25,17},{2,26},{10... | collective-permute-start | bytes 786440 | tf_op jit(solution)/shard_map/ppermute | solution.py:198
  185.5 1.9 collective-permute-start.10
  187.5 0.1 pad_add_fusion.src_ref
  187.5 1.3 collective-permute-done.8.w1_ref
  188.8 1.6 collective-permute-done.9.w2_ref
  190.5 4.6 %collective-permute-done.10.w3_ref = bf16[512,256]{1,0:T(8,128)(2,1)S(1)} collective-permute-done((bf16[512,256]{1,0:T(8,128)(2,1)S(1)}, bf16[512,256]{1,0:T(8,128)(2,1)S(1)}, u32[]{:S(2)}, u32[]{:S(2)}) %collective-permute-start.10) | collective-permute-done | bytes 262176 | tf_op jit(solution)/shard_map/ppermute | solution.py:198
  195.1 3.6 %all-to-all-done.5.m_ref = bf16[4,2,192,256]{3,2,1,0:T(8,128)(2,1)S(1)} async-done(((bf16[4,2,192,256]{3,2,1,0:T(8,128)(2,1)}), bf16[4,2,192,256]{3,2,1,0:T(8,128)(2,1)S(1)}, u32[]{:S(2)}, u32[]{:S(2)}) %all-to-all-start.5) | async-done | bytes 786464 | tf_op jit(solution)/shard_map/all_to_all | solution.py:40
  198.7 1.6 out.1
  (13 shorter events, 0.2 us)
Async XLA Ops:
  0.0 50.8 %copy-start = (bf16[512,256]{1,0:T(8,128)(2,1)S(1)}, bf16[512,256]{1,0:T(8,128)(2,1)}, u32[]{:S(2)}) copy-start(bf16[512,256]{1,0:T(8,128)(2,1)} %param.12) | copy-start | bytes 786436
  0.0 45.4 %copy-start.2 = (f32[2048]{0:T(1024)S(1)}, f32[2048]{0:T(1024)}, u32[]{:S(2)}) copy-start(f32[2048]{0:T(1024)} %param.10) | copy-start | bytes 24580
  0.0 45.4 %copy-start.3 = (f32[2048]{0:T(1024)S(1)}, f32[2048]{0:T(1024)}, u32[]{:S(2)}) copy-start(f32[2048]{0:T(1024)} %param.11) | copy-start | bytes 24580
  1.7 30.6 %all-to-all-start = ((bf16[4,192,256]{2,1,0:T(8,128)(2,1)}), bf16[4,192,256]{2,1,0:T(8,128)(2,1)S(1)}, u32[]{:S(2)}, u32[]{:S(2)}) async-start(bf16[4,192,256]{2,1,0:T(8,128)(2,1)} %broadcast_in_dim.89), calls=%async_computation | async-start | bytes 786432 | tf_op jit(solution)/shard_map/all_to_all | solution.py:40
  15.3 3.7 %collective-permute-start = (f32[16,256]{1,0:T(8,128)S(1)}, f32[16,256]{1,0:T(8,128)S(1)}, u32[]{:S(2)}, u32[]{:S(2)}) collective-permute-start(f32[16,256]{1,0:T(8,128)S(1)} %broadcast_in_dim.90), channel_id=1, source_target_pairs={{0,32},{32,0},{1,33},{33,1},{2,34},{34,2},{3,35},{35,3},{4,36},{36... | collective-permute-start | bytes 49160 | tf_op jit(solution)/shard_map/ppermute | solution.py:206
  32.3 13.1 %collective-permute-start.1 = (bf16[4,192,256]{2,1,0:T(8,128)(2,1)S(1)}, bf16[4,192,256]{2,1,0:T(8,128)(2,1)S(1)}, u32[]{:S(2)}, u32[]{:S(2)}) collective-permute-start(bf16[4,192,256]{2,1,0:T(8,128)(2,1)S(1)} %all-to-all-done.near_ref), channel_id=1, source_target_pairs={{0,1},{1,0},{2,3},{3,2},{4,5},{5,4},{6,7},{7,6},{8,9},{9,8},{10,11... | collective-permute-start | bytes 1179656 | tf_op jit(solution)/shard_map/ppermute | solution.py:211
  45.4 5.5 %copy-start.5 = (bf16[512,256]{1,0:T(8,128)(2,1)S(1)}, bf16[512,256]{1,0:T(8,128)(2,1)}, u32[]{:S(2)}) copy-start(bf16[512,256]{1,0:T(8,128)(2,1)} %param.14) | copy-start | bytes 786436
  45.4 5.5 %copy-start.6 = (bf16[512,256]{1,0:T(8,128)(2,1)S(1)}, bf16[512,256]{1,0:T(8,128)(2,1)}, u32[]{:S(2)}) copy-start(bf16[512,256]{1,0:T(8,128)(2,1)} %param.13) | copy-start | bytes 786436
  46.2 28.0 %collective-permute-start.2 = (bf16[4,192,512]{2,1,0:T(8,128)(2,1)S(1)}, bf16[4,192,512]{2,1,0:T(8,128)(2,1)S(1)}, u32[]{:S(2)}, u32[]{:S(2)}) collective-permute-start(bf16[4,192,512]{2,1,0:T(8,128)(2,1)S(1)} %norm.1.own_ref), channel_id=1, source_target_pairs={{0,32},{32,0},{1,33},{33,1},{2,34},{34,2},{3,35},{35,3},{4,36},{36... | collective-permute-start | bytes 2359304 | tf_op jit(solution)/shard_map/ppermute | solution.py:220
  51.0 13.8 %collective-permute-start.3 = (bf16[512,384]{1,0:T(8,128)(2,1)S(1)}, bf16[512,384]{1,0:T(8,128)(2,1)S(1)}, u32[]{:S(2)}, u32[]{:S(2)}) collective-permute-start(bf16[512,384]{1,0:T(8,128)(2,1)S(1)} %pad_maximum_fusion.w0_ref), channel_id=1, source_target_pairs={{0,8},{8,16},{16,24},{24,0},{1,9},{9,17},{17,25},{25,1},{2,10},{10... | collective-permute-start | bytes 1179656 | tf_op jit(solution)/shard_map/ppermute | solution.py:196
  54.1 12.3 %collective-permute-start.4 = (bf16[512,384]{1,0:T(8,128)(2,1)S(1)}, bf16[512,384]{1,0:T(8,128)(2,1)S(1)}, u32[]{:S(2)}, u32[]{:S(2)}) collective-permute-start(bf16[512,384]{1,0:T(8,128)(2,1)S(1)} %pad_maximum_fusion.w0_ref), channel_id=1, source_target_pairs={{0,24},{8,0},{16,8},{24,16},{1,25},{9,1},{17,9},{25,17},{2,26},{10... | collective-permute-start | bytes 1179656 | tf_op jit(solution)/shard_map/ppermute | solution.py:196
  57.5 16.7 %collective-permute-start.5 = (bf16[512,384]{1,0:T(8,128)(2,1)S(1)}, bf16[512,384]{1,0:T(8,128)(2,1)S(1)}, u32[]{:S(2)}, u32[]{:S(2)}) collective-permute-start(bf16[512,384]{1,0:T(8,128)(2,1)S(1)} %pad_maximum_fusion.w0_ref), channel_id=1, source_target_pairs={{0,16},{8,24},{16,0},{24,8},{1,17},{9,25},{17,1},{25,9},{2,18},{10... | collective-permute-start | bytes 1179656 | tf_op jit(solution)/shard_map/ppermute | solution.py:196
  76.4 15.7 %copy-start.4 = (bf16[2,208,256]{2,1,0:T(8,128)(2,1)}, bf16[2,208,256]{2,1,0:T(8,128)(2,1)S(1)}, u32[]{:S(2)}) copy-start(bf16[2,208,256]{2,1,0:T(8,128)(2,1)S(1)} %get-tuple-element.16) | copy-start | bytes 638980
  92.1 19.6 %all-to-all-start.1 = ((bf16[4,384,128]{2,1,0:T(8,128)(2,1)}), bf16[4,384,128]{2,1,0:T(8,128)(2,1)S(1)}, u32[]{:S(2)}, u32[]{:S(2)}) async-start(bf16[4,384,128]{2,1,0:T(8,128)(2,1)} %get-tuple-element.15), calls=%async_computation.1 | async-start | bytes 786432 | tf_op jit(solution)/shard_map/all_to_all | solution.py:234
  95.9 15.8 %collective-permute-start.6 = (bf16[2,208,256]{2,1,0:T(8,128)(2,1)}, bf16[2,208,256]{2,1,0:T(8,128)(2,1)S(1)}, u32[]{:S(2)}, u32[]{:S(2)}) collective-permute-start(bf16[2,208,256]{2,1,0:T(8,128)(2,1)} %copy-done.4), channel_id=1, source_target_pairs={{0,64},{1,65},{2,66},{3,67},{4,68},{5,69},{6,70},{7,71},{64,0},{65... | collective-permute-start | bytes 638984 | tf_op jit(solution)/shard_map/ppermute | solution.py:233
  112.7 12.2 %all-to-all-start.3 = ((bf16[4,2,208,256]{3,2,1,0:T(8,128)(2,1)}), bf16[4,2,208,256]{3,2,1,0:T(8,128)(2,1)S(1)}, u32[]{:S(2)}, u32[]{:S(2)}) async-start(bf16[4,2,208,256]{3,2,1,0:T(8,128)(2,1)} %broadcast_in_dim.98), calls=%async_computation.3 | async-start | bytes 1703936 | tf_op jit(solution)/shard_map/all_to_all | solution.py:40
  131.8 24.2 %all-to-all-start.4 = ((bf16[8,208,128]{2,1,0:T(8,128)(2,1)}), bf16[8,208,128]{2,1,0:T(8,128)(2,1)S(1)}, u32[]{:S(2)}, u32[]{:S(2)}) async-start(bf16[8,208,128]{2,1,0:T(8,128)(2,1)} %far.1), calls=%async_computation.4 | async-start | bytes 851968 | tf_op jit(solution)/shard_map/all_to_all | solution.py:268
  156.7 22.3 %copy-start.1 = (bf16[512,256]{1,0:T(8,128)(2,1)S(1)}, bf16[512,256]{1,0:T(8,128)(2,1)}, u32[]{:S(2)}) copy-start(bf16[512,256]{1,0:T(8,128)(2,1)} %w0_ref.1) | copy-start | bytes 786436
  156.7 9.4 %collective-permute-start.7 = (bf16[192,256]{1,0:T(8,128)(2,1)S(1)}, bf16[192,256]{1,0:T(8,128)(2,1)S(1)}, u32[]{:S(2)}, u32[]{:S(2)}) collective-permute-start(bf16[192,256]{1,0:T(8,128)(2,1)S(1)} %pad_maximum_fusion.2), channel_id=1, source_target_pairs={{0,4},{4,0},{1,5},{5,1},{2,6},{6,2},{3,7},{7,3},{8,12},{12,8},{9,1... | collective-permute-start | bytes 294920 | tf_op jit(solution)/shard_map/ppermute | solution.py:275
  167.1 31.6 %all-to-all-start.5 = ((bf16[4,2,192,256]{3,2,1,0:T(8,128)(2,1)}), bf16[4,2,192,256]{3,2,1,0:T(8,128)(2,1)S(1)}, u32[]{:S(2)}, u32[]{:S(2)}) async-start(bf16[4,2,192,256]{3,2,1,0:T(8,128)(2,1)} %broadcast_in_dim.99), calls=%async_computation.5 | async-start | bytes 1572864 | tf_op jit(solution)/shard_map/all_to_all | solution.py:40
  179.0 9.8 %collective-permute-start.8 = (bf16[512,256]{1,0:T(8,128)(2,1)S(1)}, bf16[512,256]{1,0:T(8,128)(2,1)S(1)}, u32[]{:S(2)}, u32[]{:S(2)}) collective-permute-start(bf16[512,256]{1,0:T(8,128)(2,1)S(1)} %copy-done.1), channel_id=1, source_target_pairs={{0,8},{8,16},{16,24},{24,0},{1,9},{9,17},{17,25},{25,1},{2,10},{10... | collective-permute-start | bytes 786440 | tf_op jit(solution)/shard_map/ppermute | solution.py:198
  181.2 9.3 %collective-permute-start.9 = (bf16[512,256]{1,0:T(8,128)(2,1)S(1)}, bf16[512,256]{1,0:T(8,128)(2,1)S(1)}, u32[]{:S(2)}, u32[]{:S(2)}) collective-permute-start(bf16[512,256]{1,0:T(8,128)(2,1)S(1)} %copy-done.1), channel_id=1, source_target_pairs={{0,24},{8,0},{16,8},{24,16},{1,25},{9,1},{17,9},{25,17},{2,26},{10... | collective-permute-start | bytes 786440 | tf_op jit(solution)/shard_map/ppermute | solution.py:198
  185.5 9.6 %collective-permute-start.10 = (bf16[512,256]{1,0:T(8,128)(2,1)S(1)}, bf16[512,256]{1,0:T(8,128)(2,1)S(1)}, u32[]{:S(2)}, u32[]{:S(2)}) collective-permute-start(bf16[512,256]{1,0:T(8,128)(2,1)S(1)} %copy-done.1), channel_id=1, source_target_pairs={{0,16},{8,24},{16,0},{24,8},{1,17},{9,25},{17,1},{25,9},{2,18},{10... | collective-permute-start | bytes 786440 | tf_op jit(solution)/shard_map/ppermute | solution.py:198

commit v2 on v1

--- a/solution.py
+++ b/solution.py
@@ -67,7 +67,7 @@
 
 
 def qkv_kernel(
-    src_ref, core_ref, own_ref, oth_ref, w0_ref, w1_ref, w2_ref, w3_ref, cnt_ref, q_ref, kv_ref, kvs_ref
+    src_ref, core_ref, own_ref, oth_ref, w0_ref, w1_ref, w2_ref, w3_ref, cnt_ref, q_ref, kv_ref
 ):
     for c, n_ref in enumerate((own_ref, oth_ref)):
         acc = jnp.zeros((ROWS, 384), F32)
@@ -79,8 +79,6 @@
         count = cnt_ref[c].astype(BF16)
         for copy in range(4):
             q_ref[copy, pl.ds(at, ROWS), :] = query
-            kvs_ref[copy, c, :ROWS, :] = pair
-            kvs_ref[copy, c, ROWS:, :] = count
         kv_ref[c, :ROWS, :] = pair
         kv_ref[c, ROWS:, :] = count
 
@@ -89,12 +87,19 @@
 TN = (((0,), (0,)), ((), ()))
 
 
-def scan_keys(query, kv_ref, s_ref, acc_ref, best, total):
+def scan_keys(query, kv_refs, s_ref, acc_ref, best, total):
     width = query.shape[0]
-    blocks = kv_ref.shape[0]
     before = best
 
-    def first(b, best):
+    def over(body, carry):
+        base = 0
+        for kv_ref in kv_refs:
+            for b in range(kv_ref.shape[0]):
+                carry = body(kv_ref, b, base + b, carry)
+            base += kv_ref.shape[0]
+        return carry
+
+    def first(kv_ref, b, at, best):
         for c in range(2):
             keys = kv_ref[b, c, :ROWS, :128]
             score = lax.dot_general(keys, query, NT, preferred_element_type=F32)
@@ -102,18 +107,18 @@
             live = kv_ref[b, c, pl.ds(ROWS, 1), :].astype(F32)
             live = jnp.concatenate([live] * (width // 256), axis=1)
             score = jnp.where(row < live, score, -1e30)
-            s_ref[pl.ds((b * 2 + c) * ROWS, ROWS), :] = score
+            s_ref[pl.ds((at * 2 + c) * ROWS, ROWS), :] = score
             best = jnp.maximum(best, jnp.max(score, axis=0, keepdims=True))
         return best
 
-    best = lax.fori_loop(0, blocks, first, best)
+    best = over(first, best)
     shrink = jnp.exp(before - best)
     total = total * shrink
     acc_ref[...] = acc_ref[...] * shrink
 
-    def second(b, total):
+    def second(kv_ref, b, at, total):
         for c in range(2):
-            weight = jnp.exp(s_ref[pl.ds((b * 2 + c) * ROWS, ROWS), :] - best)
+            weight = jnp.exp(s_ref[pl.ds((at * 2 + c) * ROWS, ROWS), :] - best)
             total = total + jnp.sum(weight, axis=0, keepdims=True)
             values = kv_ref[b, c, :ROWS, 128:256]
             acc_ref[...] += lax.dot_general(
@@ -121,15 +126,15 @@
             )
         return total
 
-    return best, lax.fori_loop(0, blocks, second, total)
-
-
-def near_kernel(q_ref, kv_ref, acc_ref, stat_ref, s_ref):
+    return best, over(second, total)
+
+
+def near_kernel(q_ref, k0_ref, k1_ref, k2_ref, k3_ref, acc_ref, stat_ref, s_ref):
     width = q_ref.shape[0]
     acc_ref[...] = jnp.zeros_like(acc_ref)
     best, total = scan_keys(
         q_ref[...],
-        kv_ref,
+        (k0_ref, k1_ref, k2_ref, k3_ref),
         s_ref,
         acc_ref,
         jnp.full((1, width), -1e30, F32),
@@ -144,7 +149,7 @@
     width = q_ref.shape[0]
     acc_ref[...] = part_ref[...]
     best, total = scan_keys(
-        q_ref[...], kv_ref, s_ref, acc_ref, stat_ref[0:1, :], stat_ref[1:2, :]
+        q_ref[...], (kv_ref,), s_ref, acc_ref, stat_ref[0:1, :], stat_ref[1:2, :]
     )
     mixed = (acc_ref[...] / total).T.astype(BF16)
     level = best + jnp.log(total)
@@ -166,17 +171,16 @@
             out_ref[2 * x + c, ROWS : ROWS + 16, :] = stats
 
 
-def out_kernel(src_ref, half_ref, m_ref, w0_ref, w1_ref, w2_ref, w3_ref, out_ref):
-    acc = jnp.zeros(out_ref.shape, F32)
-    for s, w_ref in enumerate((w0_ref, w1_ref, w2_ref, w3_ref)):
-        for step in range(2):
-            at = src_ref[s] + step
-            acc = acc + jnp.dot(
-                m_ref[at % 4, half_ref[0] ^ (at // 4)],
-                w_ref[step * 256 : (step + 1) * 256, :],
-                preferred_element_type=F32,
-            )
-    out_ref[...] = acc
+def out_kernel(
+    src_ref, grp_ref, m0_ref, m1_ref, m2_ref, m3_ref, w0_ref, w1_ref, w2_ref, w3_ref, own_ref, away_ref, w_ref
+):
+    for s, piece_ref in enumerate((w0_ref, w1_ref, w2_ref, w3_ref)):
+        w_ref[src_ref[s]] = piece_ref[...]
+    acc = jnp.zeros((ROWS, 512), F32)
+    for k, m_ref in enumerate((m0_ref, m1_ref, m2_ref, m3_ref)):
+        acc = acc + jnp.dot(m_ref[...], w_ref[grp_ref[k]], preferred_element_type=F32)
+    own_ref[...] = acc[:, :256]
+    away_ref[...] = acc[:, 256:].astype(BF16)
 
 
 VMEM = pl.BlockSpec(memory_space=pltpu.VMEM)
@@ -194,13 +198,12 @@
     )
     weights = [w_own]
     weights += [lax.ppermute(w_own, "row", ring(4, s)) for s in SHIFTS[1:]]
-    outward = [w_output]
-    outward += [lax.ppermute(w_output, "row", ring(4, s)) for s in SHIFTS[1:]]
     source = jnp.stack([(row - s) % 4 for s in SHIFTS]).astype(jnp.int32)
-    chunks = jnp.stack([(row - s) % 4 * 2 for s in SHIFTS]).astype(jnp.int32)
+    place = lax.axis_index(("c2", "c1"))
+    group = jnp.stack([place ^ (k % 4) for k in range(8)]).astype(jnp.int32)
+    chunks = jnp.stack([(row - s + 8) % 4 for s in SHIFTS]).astype(jnp.int32)
     core = core.astype(jnp.int32)[None]
     parity = lax.axis_index("c0").astype(jnp.int32)[None]
-    half = lax.axis_index("c2").astype(jnp.int32)[None]
 
     live = jnp.full((16, 256), jnp.sum((visible >= 0).astype(F32)), F32)
     counts = jnp.stack([live, lax.ppermute(live, "core", ring(2, 1))])
@@ -209,6 +212,9 @@
     near = spread(patches, ("c2", "c1"), 4)
     near, counts = lax.optimization_barrier((near, counts))
     side = lax.ppermute(near, "c0", ring(2, 1))
+    keep = lax.dynamic_slice_in_dim(w_output, parity[0] * 256, 256, 0)
+    give = lax.dynamic_slice_in_dim(w_output, (1 - parity[0]) * 256, 256, 0)
+    taken = lax.ppermute(give, "c0", ring(2, 1))
     own = pl.pallas_call(
         norm_kernel,
         out_shape=jax.ShapeDtypeStruct((4, ROWS, 512), BF16),
@@ -218,24 +224,24 @@
         name="norm",
     )(parity, near, side, pos, ln_gain[None, :], ln_bias[None, :])
     other = lax.ppermute(own, "core", ring(2, 1))
-    query, kv, near_kv = pl.pallas_call(
+    query, kv = pl.pallas_call(
         qkv_kernel,
         out_shape=(
             jax.ShapeDtypeStruct((4, 2 * ROWS, 128), BF16),
             jax.ShapeDtypeStruct((2, ROWS + 16, 256), BF16),
-            jax.ShapeDtypeStruct((4, 2, ROWS + 16, 256), BF16),
         ),
         in_specs=[SMEM] * 2 + [VMEM] * 7,
-        out_specs=(VMEM, VMEM, VMEM),
+        out_specs=(VMEM, VMEM),
         compiler_params=PARAMS,
         name="qkv",
     )(source, core, own, other, *weights, counts)
     far_kv = lax.ppermute(kv, ("zh", "c2", "c1", "c0"), ring(16, 8))
     query = lax.all_to_all(query, "row", 0, 0).reshape(8 * ROWS, 128)
-    near_kv = lax.all_to_all(near_kv, "y", 0, 0)
-    far_kv, _ = lax.optimization_barrier((far_kv, near_kv))
+    near_kv = [kv[None]]
+    near_kv += [lax.ppermute(kv, "y", ring(4, s))[None] for s in SHIFTS[1:]]
     far_kv = spread(far_kv, "y", 4)
     kv_spec = pl.BlockSpec((4, 2, ROWS + 16, 256), lambda i: (0, 0, 0, 0))
+    one_spec = pl.BlockSpec((1, 2, ROWS + 16, 256), lambda i: (0, 0, 0, 0))
     q_spec = pl.BlockSpec((4 * ROWS, 128), lambda i: (i, 0))
     acc_spec = pl.BlockSpec((128, 4 * ROWS), lambda i: (0, i))
     stat_spec = pl.BlockSpec((8, 4 * ROWS), lambda i: (0, i))
@@ -246,12 +252,12 @@
             jax.ShapeDtypeStruct((128, 8 * ROWS), F32),
             jax.ShapeDtypeStruct((8, 8 * ROWS), F32),
         ),
-        in_specs=[q_spec, kv_spec],
+        in_specs=[q_spec] + [one_spec] * 4,
         out_specs=(acc_spec, stat_spec),
         scratch_shapes=[pltpu.VMEM((8 * ROWS, 4 * ROWS), F32)],
         compiler_params=PARAMS,
         name="near",
-    )(query, near_kv)
+    )(query, *near_kv)
     part = pl.pallas_call(
         far_kernel,
         grid=(2,),
@@ -265,6 +271,9 @@
         compiler_params=PARAMS,
         name="far",
     )(query, far_kv, acc, stat)
+    outward = [jnp.concatenate([keep, taken], axis=1)]
+    outward += [lax.ppermute(outward[0], "row", ring(4, s)) for s in SHIFTS[1:3]]
+    outward.append(lax.ppermute(outward[0], "row", ring(4, SHIFTS[3])))
     part = lax.all_to_all(part, ("row", "core"), 0, 0).reshape(4, 2, ROWS + 16, 128)
     stats = part[:, :, ROWS : ROWS + 9, :].astype(F32).reshape(4, 2, 3, 2 * ROWS).sum(axis=2)
     stats = lax.dynamic_slice_in_dim(stats, core[0] * ROWS, ROWS, 2)
@@ -272,17 +281,23 @@
     share = share / jnp.sum(share, axis=0, keepdims=True)
     mixed = jnp.sum(part[:, :, :ROWS, :].astype(F32) * share[..., None], axis=0)
     mixed = jnp.concatenate([mixed[0], mixed[1]], axis=1).astype(BF16)
-    swapped = lax.ppermute(mixed, "c2", ring(2, 1))
-    mixed = jnp.stack([mixed, swapped])
-    mixed = spread(mixed, ("c1", "c0"), 4)
-    return pl.pallas_call(
+    heads = [mixed]
+    for k in (1, 2, 3):
+        pairs = [(g, g ^ k) for g in range(4)]
+        heads.append(lax.ppermute(mixed, ("c2", "c1"), pairs))
+    own, away = pl.pallas_call(
         out_kernel,
-        out_shape=jax.ShapeDtypeStruct((ROWS, 256), F32),
-        in_specs=[SMEM] * 2 + [VMEM] * 5,
-        out_specs=VMEM,
+        out_shape=(
+            jax.ShapeDtypeStruct((ROWS, 256), F32),
+            jax.ShapeDtypeStruct((ROWS, 256), BF16),
+        ),
+        in_specs=[SMEM] * 2 + [VMEM] * 8,
+        out_specs=(VMEM, VMEM),
+        scratch_shapes=[pltpu.VMEM((4, 256, 512), BF16)],
         compiler_params=PARAMS,
         name="out",
-    )(chunks, half, mixed, *outward)
+    )(chunks, group, *heads, *outward)
+    return own + lax.ppermute(away, "c0", ring(2, 1)).astype(F32)
 
 
 def solution(mesh):

time: 201 us -> 206 us (1.025)
  blocking collectives: 15.7 us -> 0 us
  starting transfers between devices: 91.4 us -> 104 us
  waiting for transfers between devices: 62.1 us -> 71.1 us
  Pallas kernels: 17.6 us -> 15.2 us
    ppermute x4 -> x11, starting transfers between devices: 10.5 us -> 42.9 us  [the longest x3 14.7 us: sublayer(): heads.append(lax.ppermute(mixed, ('c2', 'c1'), pairs))]
    all_to_all x1 -> x0, blocking collectives: 15.7 us -> none  [sublayer(): near_kv = lax.all_to_all(near_kv, 'y', 0, 0)]
    ppermute x4 -> x11, waiting for transfers between devices: 14.9 us -> 29.9 us  [the longest x3 13.5 us: sublayer(): heads.append(lax.ppermute(mixed, ('c2', 'c1'), pairs))]
    all_to_all x3 -> x2, starting transfers between devices: 27.2 us -> 15.9 us  [spread(): return lax.all_to_all(copies, axes, 0, 0)]
    all_to_all x1, starting transfers between devices: 16.2 us -> 7.24 us  [sublayer(): lax.all_to_all(part, ('row', 'core'), 0, 0).reshape(4, 2, ROWS + 16, 128)]
    ppermute x1, waiting for transfers between devices: 5.1 us -> 13.4 us  [sublayer(): far_kv = lax.ppermute(kv, ('zh', 'c2', 'c1', 'c0'), ring(16, 8))]
    all_to_all x1, waiting for transfers between devices: 8.01 us -> 0.01 us  [sublayer(): lax.all_to_all(part, ('row', 'core'), 0, 0).reshape(4, 2, ROWS + 16, 128)]
    all_to_all x3 -> x2, waiting for transfers between devices: 19 us -> 12.6 us  [spread(): return lax.all_to_all(copies, axes, 0, 0)]
  transfers between devices with their start and end apart: 16 -> 22, of which waited for: 14 -> 12; matrix products, arithmetic and copies ran while one was open for 4% -> 5% of each run, Pallas kernels for 3% -> 2%
where the time goes in v2:
time: 206 us; the launch traced here: 205 us
  starting transfers between devices  104 us (50%)
  waiting for transfers between devices  71.1 us (35%)
  Pallas kernels  15.2 us (7%)
  other arithmetic  8.9 us (4%)
  local copies, waits for them, and re-layouts  4.89 us (2%)
    all_to_all x2, starting transfers between devices, spread(): return lax.all_to_all(copies, axes, 0, 0)  15.9 us
    ppermute x3, starting transfers between devices, sublayer(): heads.append(lax.ppermute(mixed, ('c2', 'c1'), pairs))  14.7 us
    ppermute x3, waiting for transfers between devices, sublayer(): heads.append(lax.ppermute(mixed, ('c2', 'c1'), pairs))  13.5 us
    ppermute x1, waiting for transfers between devices, sublayer(): far_kv = lax.ppermute(kv, ('zh', 'c2', 'c1', 'c0'), ring(16, 8))  13.4 us
    ppermute x3, waiting for transfers between devices, sublayer(): weights += [lax.ppermute(w_own, 'row', ring(4, s)) for s in SHIFTS[1:]]  13.1 us
    all_to_all x2, waiting for transfers between devices, spread(): return lax.all_to_all(copies, axes, 0, 0)  12.6 us
    ppermute x1, starting transfers between devices, sublayer(): far_kv = lax.ppermute(kv, ('zh', 'c2', 'c1', 'c0'), ring(16, 8))  10.8 us
    ppermute x3, starting transfers between devices, sublayer(): near_kv += [lax.ppermute(kv, 'y', ring(4, s))[None] for s in SHIFTS[1:]]  10.3 us
  transfers between devices with their start and end apart: 22, of which 12 were waited for; matrix products, arithmetic and copies ran while one was open for 5% of the time, Pallas kernels for 2%

profile of v2, /device:TPU:1, one launch (start us, length us, event | category | flops | bytes accessed | tf_op | source)
XLA Modules:
  0.0 204.9 jit_solution(12675959441332649169)
XLA Ops:
  0.0 1.7 broadcast_in_dim.91
  1.7 11.7 %all-to-all-start = ((bf16[4,192,256]{2,1,0:T(8,128)(2,1)}), bf16[4,192,256]{2,1,0:T(8,128)(2,1)S(1)}, u32[]{:S(2)}, u32[]{:S(2)}) async-start(bf16[4,192,256]{2,1,0:T(8,128)(2,1)} %broadcast_in_dim.91), calls=%async_computation | async-start | bytes 786432 | tf_op jit(solution)/shard_map/all_to_all | solution.py:40
  13.4 1.3 fusion.17
  14.7 0.6 broadcast_in_dim.92
  15.4 2.9 %collective-permute-start = (f32[16,256]{1,0:T(8,128)S(1)}, f32[16,256]{1,0:T(8,128)S(1)}, u32[]{:S(2)}, u32[]{:S(2)}) collective-permute-start(f32[16,256]{1,0:T(8,128)S(1)} %broadcast_in_dim.92), channel_id=1, source_target_pairs={{0,32},{32,0},{1,33},{33,1},{2,34},{34,2},{3,35},{35,3},{4,36},{36... | collective-permute-start | bytes 49160 | tf_op jit(solution)/shard_map/ppermute | solution.py:209
  18.3 0.7 fusion.18
  19.0 0.1 collective-permute-done
  19.1 0.6 stack.71.cnt_ref
  19.7 12.6 %all-to-all-done.near_ref = bf16[4,192,256]{2,1,0:T(8,128)(2,1)S(1)} async-done(((bf16[4,192,256]{2,1,0:T(8,128)(2,1)}), bf16[4,192,256]{2,1,0:T(8,128)(2,1)S(1)}, u32[]{:S(2)}, u32[]{:S(2)}) %all-to-all-start) | async-done | bytes 393248 | tf_op jit(solution)/shard_map/all_to_all | solution.py:40
  32.3 5.7 %collective-permute-start.1 = (bf16[4,192,256]{2,1,0:T(8,128)(2,1)S(1)}, bf16[4,192,256]{2,1,0:T(8,128)(2,1)S(1)}, u32[]{:S(2)}, u32[]{:S(2)}) collective-permute-start(bf16[4,192,256]{2,1,0:T(8,128)(2,1)S(1)} %all-to-all-done.near_ref), channel_id=1, source_target_pairs={{0,1},{1,0},{2,3},{3,2},{4,5},{5,4},{6,7},{7,6},{8,9},{9,8},{10,11... | collective-permute-start | bytes 1179656 | tf_op jit(solution)/shard_map/ppermute | solution.py:214
  38.0 5.3 %add_sine_fusion.pos_ref = f32[192,2048]{1,0:T(8,128)S(1)} fusion(f32[2048]{0:T(1024)S(1)} %get-tuple-element.29, f32[2048]{0:T(1024)S(1)} %get-tuple-element.28, f32[192]{0:T(256)S(1)} %get-tuple-element.27, f32[192]{0:T(256)S(1)} %get-tuple-element.26, f32[192]{0:T(256)S(1)} %get-tuple-element.25, pred[2048]{0:T(1024)(128)(4,1)S(1)} %get-tuple-element.30, ...), kind=kLoop, calls=%fused_computation | loop fusion | flops 1572864 | bytes 1595648 | tf_op jit(solution)/shard_map/sin | solution.py:35
  43.4 2.0 collective-permute-done.1.side_ref
  45.4 0.8 norm.1.own_ref
  46.2 4.6 %collective-permute-start.2 = (bf16[4,192,512]{2,1,0:T(8,128)(2,1)S(1)}, bf16[4,192,512]{2,1,0:T(8,128)(2,1)S(1)}, u32[]{:S(2)}, u32[]{:S(2)}) collective-permute-start(bf16[4,192,512]{2,1,0:T(8,128)(2,1)S(1)} %norm.1.own_ref), channel_id=1, source_target_pairs={{0,32},{32,0},{1,33},{33,1},{2,34},{34,2},{3,35},{35,3},{4,36},{36... | collective-permute-start | bytes 2359304 | tf_op jit(solution)/shard_map/ppermute | solution.py:226
  50.9 0.1 pad_maximum_fusion.w0_ref
  51.0 3.1 %collective-permute-start.3 = (bf16[512,384]{1,0:T(8,128)(2,1)S(1)}, bf16[512,384]{1,0:T(8,128)(2,1)S(1)}, u32[]{:S(2)}, u32[]{:S(2)}) collective-permute-start(bf16[512,384]{1,0:T(8,128)(2,1)S(1)} %pad_maximum_fusion.w0_ref), channel_id=1, source_target_pairs={{0,8},{8,16},{16,24},{24,0},{1,9},{9,17},{17,25},{25,1},{2,10},{10... | collective-permute-start | bytes 1179656 | tf_op jit(solution)/shard_map/ppermute | solution.py:200
  54.1 3.4 %collective-permute-start.4 = (bf16[512,384]{1,0:T(8,128)(2,1)S(1)}, bf16[512,384]{1,0:T(8,128)(2,1)S(1)}, u32[]{:S(2)}, u32[]{:S(2)}) collective-permute-start(bf16[512,384]{1,0:T(8,128)(2,1)S(1)} %pad_maximum_fusion.w0_ref), channel_id=1, source_target_pairs={{0,24},{8,0},{16,8},{24,16},{1,25},{9,1},{17,9},{25,17},{2,26},{10... | collective-permute-start | bytes 1179656 | tf_op jit(solution)/shard_map/ppermute | solution.py:200
  57.5 3.4 %collective-permute-start.5 = (bf16[512,384]{1,0:T(8,128)(2,1)S(1)}, bf16[512,384]{1,0:T(8,128)(2,1)S(1)}, u32[]{:S(2)}, u32[]{:S(2)}) collective-permute-start(bf16[512,384]{1,0:T(8,128)(2,1)S(1)} %pad_maximum_fusion.w0_ref), channel_id=1, source_target_pairs={{0,16},{8,24},{16,0},{24,8},{1,17},{9,25},{17,1},{25,9},{2,18},{10... | collective-permute-start | bytes 1179656 | tf_op jit(solution)/shard_map/ppermute | solution.py:200
  61.0 0.1 pad_add_fusion.1.src_ref
  61.1 3.7 %collective-permute-done.3.w1_ref = bf16[512,384]{1,0:T(8,128)(2,1)S(1)} collective-permute-done((bf16[512,384]{1,0:T(8,128)(2,1)S(1)}, bf16[512,384]{1,0:T(8,128)(2,1)S(1)}, u32[]{:S(2)}, u32[]{:S(2)}) %collective-permute-start.3) | collective-permute-done | bytes 393248 | tf_op jit(solution)/shard_map/ppermute | solution.py:200
  64.8 1.6 collective-permute-done.4.w2_ref
  66.4 7.8 %collective-permute-done.5.w3_ref = bf16[512,384]{1,0:T(8,128)(2,1)S(1)} collective-permute-done((bf16[512,384]{1,0:T(8,128)(2,1)S(1)}, bf16[512,384]{1,0:T(8,128)(2,1)S(1)}, u32[]{:S(2)}, u32[]{:S(2)}) %collective-permute-start.5) | collective-permute-done | bytes 393248 | tf_op jit(solution)/shard_map/ppermute | solution.py:200
  74.2 0.0 collective-permute-done.2.oth_ref
  74.2 2.3 %qkv.1 = (bf16[4,384,128]{2,1,0:T(8,128)(2,1)}, bf16[2,208,256]{2,1,0:T(8,128)(2,1)S(1)}) custom-call(s32[4]{0:T(128)S(1)} %pad_add_fusion.1.src_ref, s32[1]{0:T(128)} %bitcast.12.core_ref, bf16[4,192,512]{2,1,0:T(8,128)(2,1)S(1)} %norm.1.own_ref, bf16[4,192,512]{2,1,0:T(8,128)(2,1)S(1)} %collective-permute-done.2.oth_ref, ...), custom_call_target="tpu_custom_call" | custom-call | tf_op jit(solution)/shard_map/qkv/pallas_call | solution.py:227
  76.4 0.7 copy-done.1
  77.1 4.4 %all-to-all-start.1 = ((bf16[4,384,128]{2,1,0:T(8,128)(2,1)}), bf16[4,384,128]{2,1,0:T(8,128)(2,1)S(1)}, u32[]{:S(2)}, u32[]{:S(2)}) async-start(bf16[4,384,128]{2,1,0:T(8,128)(2,1)} %get-tuple-element.15), calls=%async_computation.1 | async-start | bytes 786432 | tf_op jit(solution)/shard_map/all_to_all | solution.py:239
  81.5 10.8 %collective-permute-start.6 = (bf16[2,208,256]{2,1,0:T(8,128)(2,1)}, bf16[2,208,256]{2,1,0:T(8,128)(2,1)S(1)}, u32[]{:S(2)}, u32[]{:S(2)}) collective-permute-start(bf16[2,208,256]{2,1,0:T(8,128)(2,1)} %copy-done.1), channel_id=1, source_target_pairs={{0,64},{1,65},{2,66},{3,67},{4,68},{5,69},{6,70},{7,71},{64,0},{65... | collective-permute-start | bytes 638984 | tf_op jit(solution)/shard_map/ppermute | solution.py:238
  92.3 13.4 %collective-permute-done.6 = bf16[2,208,256]{2,1,0:T(8,128)(2,1)S(1)} collective-permute-done((bf16[2,208,256]{2,1,0:T(8,128)(2,1)}, bf16[2,208,256]{2,1,0:T(8,128)(2,1)S(1)}, u32[]{:S(2)}, u32[]{:S(2)}) %collective-permute-start.6) | collective-permute-done | bytes 213024 | tf_op jit(solution)/shard_map/ppermute | solution.py:238
  105.8 0.0 all-to-all-done.1
  105.8 1.0 broadcast_in_dim.100
  106.8 4.2 %all-to-all-start.2 = ((bf16[4,2,208,256]{3,2,1,0:T(8,128)(2,1)}), bf16[4,2,208,256]{3,2,1,0:T(8,128)(2,1)S(1)}, u32[]{:S(2)}, u32[]{:S(2)}) async-start(bf16[4,2,208,256]{3,2,1,0:T(8,128)(2,1)} %broadcast_in_dim.100), calls=%async_computation.2 | async-start | bytes 1703936 | tf_op jit(solution)/shard_map/all_to_all | solution.py:40
  110.9 3.4 %collective-permute-start.7 = (bf16[2,208,256]{2,1,0:T(8,128)(2,1)S(1)}, bf16[2,208,256]{2,1,0:T(8,128)(2,1)S(1)}, u32[]{:S(2)}, u32[]{:S(2)}) collective-permute-start(bf16[2,208,256]{2,1,0:T(8,128)(2,1)S(1)} %copy-done.2), channel_id=1, source_target_pairs={{0,128},{128,256},{256,384},{384,0},{1,129},{129,257},{257,385},{3... | collective-permute-start | bytes 638984 | tf_op jit(solution)/shard_map/ppermute | solution.py:241
  114.3 3.1 %collective-permute-start.8 = (bf16[2,208,256]{2,1,0:T(8,128)(2,1)S(1)}, bf16[2,208,256]{2,1,0:T(8,128)(2,1)S(1)}, u32[]{:S(2)}, u32[]{:S(2)}) collective-permute-start(bf16[2,208,256]{2,1,0:T(8,128)(2,1)S(1)} %copy-done.2), channel_id=1, source_target_pairs={{0,384},{128,0},{256,128},{384,256},{1,385},{129,1},{257,129},{385... | collective-permute-start | bytes 638984 | tf_op jit(solution)/shard_map/ppermute | solution.py:241
  117.5 3.8 %collective-permute-start.9 = (bf16[2,208,256]{2,1,0:T(8,128)(2,1)S(1)}, bf16[2,208,256]{2,1,0:T(8,128)(2,1)S(1)}, u32[]{:S(2)}, u32[]{:S(2)}) collective-permute-start(bf16[2,208,256]{2,1,0:T(8,128)(2,1)S(1)} %copy-done.2), channel_id=1, source_target_pairs={{0,256},{128,384},{256,0},{384,128},{1,257},{129,385},{257,1},{385... | collective-permute-start | bytes 638984 | tf_op jit(solution)/shard_map/ppermute | solution.py:241
  121.3 3.6 %collective-permute-done.7 = bf16[2,208,256]{2,1,0:T(8,128)(2,1)S(1)} collective-permute-done((bf16[2,208,256]{2,1,0:T(8,128)(2,1)S(1)}, bf16[2,208,256]{2,1,0:T(8,128)(2,1)S(1)}, u32[]{:S(2)}, u32[]{:S(2)}) %collective-permute-start.7) | collective-permute-done | bytes 213024 | tf_op jit(solution)/shard_map/ppermute | solution.py:241
  124.9 0.0 collective-permute-done.8
  124.9 5.6 %collective-permute-done.9 = bf16[2,208,256]{2,1,0:T(8,128)(2,1)S(1)} collective-permute-done((bf16[2,208,256]{2,1,0:T(8,128)(2,1)S(1)}, bf16[2,208,256]{2,1,0:T(8,128)(2,1)S(1)}, u32[]{:S(2)}, u32[]{:S(2)}) %collective-permute-start.9) | collective-permute-done | bytes 213024 | tf_op jit(solution)/shard_map/ppermute | solution.py:241
  130.5 4.7 %near.1 = (f32[128,1536]{1,0:T(8,128)S(1)}, f32[8,1536]{1,0:T(8,128)S(1)}) custom-call(bf16[1536,128]{1,0:T(8,128)(2,1)S(1)} %bitcast.27, bf16[1,2,208,256]{3,2,1,0:T(8,128)(2,1)S(1)} %bitcast.29, bf16[1,2,208,256]{3,2,1,0:T(8,128)(2,1)S(1)} %bitcast.30, bf16[1,2,208,256]{3,2,1,0:T(8,128)(2,1)S(1)} %bitcast.31, bf16[1,2,208,256]{3,2,1,0:T(8,128)(2,1)S(1)} %bitcast.32), custom_call_target="tpu_custom_call" | custom-call | tf_op jit(solution)/shard_map/near/pallas_call | solution.py:248
  135.3 0.0 all-to-all-done.2.kv_ref
  135.3 0.0 copy-start.5
  135.3 6.4 %far.1 = bf16[8,208,128]{2,1,0:T(8,128)(2,1)} custom-call(bf16[1536,128]{1,0:T(8,128)(2,1)S(1)} %bitcast.28, bf16[4,2,208,256]{3,2,1,0:T(8,128)(2,1)S(1)} %all-to-all-done.2.kv_ref, f32[128,1536]{1,0:T(8,128)S(1)} %get-tuple-element.17.part_ref, f32[8,1536]{1,0:T(8,128)S(1)} %get-tuple-element.18.stat_ref), custom_call_target="tpu_custom_call" | custom-call | tf_op jit(solution)/shard_map/far/pallas_call | solution.py:261
  141.7 7.2 %all-to-all-start.3 = ((bf16[8,208,128]{2,1,0:T(8,128)(2,1)}), bf16[8,208,128]{2,1,0:T(8,128)(2,1)S(1)}, u32[]{:S(2)}, u32[]{:S(2)}) async-start(bf16[8,208,128]{2,1,0:T(8,128)(2,1)} %far.1), calls=%async_computation.3 | async-start | bytes 851968 | tf_op jit(solution)/shard_map/all_to_all | solution.py:277
  149.0 6.3 %collective-permute-start.13 = (bf16[256,256]{1,0:T(8,128)(2,1)S(1)}, bf16[256,256]{1,0:T(8,128)(2,1)S(1)}, u32[]{:S(2)}, u32[]{:S(2)}) collective-permute-start(bf16[256,256]{1,0:T(8,128)(2,1)S(1)} %get-tuple-element.22), channel_id=1, source_target_pairs={{0,1},{1,0},{2,3},{3,2},{4,5},{5,4},{6,7},{7,6},{8,9},{9,8},{10,11... | collective-permute-start | bytes 393224 | tf_op jit(solution)/shard_map/ppermute | solution.py:217
  155.3 0.1 stack.64.grp_ref
  155.4 3.7 %collective-permute-done.13 = bf16[256,256]{1,0:T(8,128)(2,1)S(1)} collective-permute-done((bf16[256,256]{1,0:T(8,128)(2,1)S(1)}, bf16[256,256]{1,0:T(8,128)(2,1)S(1)}, u32[]{:S(2)}, u32[]{:S(2)}) %collective-permute-start.13) | collective-permute-done | bytes 131104 | tf_op jit(solution)/shard_map/ppermute | solution.py:217
  159.1 2.9 %collective-permute-start.14 = (bf16[256,512]{1,0:T(8,128)(2,1)S(1)}, bf16[256,512]{1,0:T(8,128)(2,1)S(1)}, u32[]{:S(2)}, u32[]{:S(2)}) collective-permute-start(bf16[256,512]{1,0:T(8,128)(2,1)S(1)} %pad_maximum_fusion.1.w0_ref), channel_id=1, source_target_pairs={{0,8},{8,16},{16,24},{24,0},{1,9},{9,17},{17,25},{25,1},{2,10},{10... | collective-permute-start | bytes 786440 | tf_op jit(solution)/shard_map/ppermute | solution.py:275
  162.0 3.6 %collective-permute-start.15 = (bf16[256,512]{1,0:T(8,128)(2,1)S(1)}, bf16[256,512]{1,0:T(8,128)(2,1)S(1)}, u32[]{:S(2)}, u32[]{:S(2)}) collective-permute-start(bf16[256,512]{1,0:T(8,128)(2,1)S(1)} %pad_maximum_fusion.1.w0_ref), channel_id=1, source_target_pairs={{0,24},{8,0},{16,8},{24,16},{1,25},{9,1},{17,9},{25,17},{2,26},{10... | collective-permute-start | bytes 786440 | tf_op jit(solution)/shard_map/ppermute | solution.py:275
  165.6 3.2 %collective-permute-start.16 = (bf16[256,512]{1,0:T(8,128)(2,1)S(1)}, bf16[256,512]{1,0:T(8,128)(2,1)S(1)}, u32[]{:S(2)}, u32[]{:S(2)}) collective-permute-start(bf16[256,512]{1,0:T(8,128)(2,1)S(1)} %pad_maximum_fusion.1.w0_ref), channel_id=1, source_target_pairs={{0,16},{8,24},{16,0},{24,8},{1,17},{9,25},{17,1},{25,9},{2,18},{10... | collective-permute-start | bytes 786440 | tf_op jit(solution)/shard_map/ppermute | solution.py:276
  168.8 0.0 all-to-all-done.3
  168.9 0.1 dynamic-slice_reduce_fusion
  169.0 0.1 fusion.16
  169.1 0.1 broadcast_divide_fusion
  169.2 0.3 multiply_reduce_fusion
  169.5 1.9 collective-permute-start.10
  171.4 10.9 %collective-permute-start.11 = (bf16[192,256]{1,0:T(8,128)(2,1)S(1)}, bf16[192,256]{1,0:T(8,128)(2,1)S(1)}, u32[]{:S(2)}, u32[]{:S(2)}) collective-permute-start(bf16[192,256]{1,0:T(8,128)(2,1)S(1)} %pad_maximum_fusion.2.m0_ref), channel_id=1, source_target_pairs={{0,4},{2,6},{4,0},{6,2},{1,5},{3,7},{5,1},{7,3},{8,12},{10,14},{12... | collective-permute-start | bytes 294920 | tf_op jit(solution)/shard_map/ppermute | solution.py:287
  182.3 1.9 collective-permute-start.12
  184.3 0.1 pad_add_fusion.src_ref
  184.3 0.0 collective-permute-done.15.w2_ref
  184.3 0.0 collective-permute-done.16.w3_ref
  184.3 13.5 %collective-permute-done.11.m2_ref = bf16[192,256]{1,0:T(8,128)(2,1)S(1)} collective-permute-done((bf16[192,256]{1,0:T(8,128)(2,1)S(1)}, bf16[192,256]{1,0:T(8,128)(2,1)S(1)}, u32[]{:S(2)}, u32[]{:S(2)}) %collective-permute-start.11) | collective-permute-done | bytes 98336 | tf_op jit(solution)/shard_map/ppermute | solution.py:287
  197.9 1.0 out.1
  198.9 1.9 collective-permute-start.17
  200.8 3.4 %collective-permute-done.17 = bf16[192,256]{1,0:T(8,128)(2,1)S(1)} collective-permute-done((bf16[192,256]{1,0:T(8,128)(2,1)S(1)}, bf16[192,256]{1,0:T(8,128)(2,1)S(1)}, u32[]{:S(2)}, u32[]{:S(2)}) %collective-permute-start.17) | collective-permute-done | bytes 98336 | tf_op jit(solution)/shard_map/ppermute | solution.py:300
  204.2 0.7 convert_add_fusion
  (28 shorter events, 0.2 us)
Async XLA Ops:
  0.0 50.8 %copy-start = (bf16[512,256]{1,0:T(8,128)(2,1)S(1)}, bf16[512,256]{1,0:T(8,128)(2,1)}, u32[]{:S(2)}) copy-start(bf16[512,256]{1,0:T(8,128)(2,1)} %param.12) | copy-start | bytes 786436
  0.0 45.4 %copy-start.3 = (f32[2048]{0:T(1024)S(1)}, f32[2048]{0:T(1024)}, u32[]{:S(2)}) copy-start(f32[2048]{0:T(1024)} %param.10) | copy-start | bytes 24580
  0.0 45.4 %copy-start.4 = (f32[2048]{0:T(1024)S(1)}, f32[2048]{0:T(1024)}, u32[]{:S(2)}) copy-start(f32[2048]{0:T(1024)} %param.11) | copy-start | bytes 24580
  1.7 30.6 %all-to-all-start = ((bf16[4,192,256]{2,1,0:T(8,128)(2,1)}), bf16[4,192,256]{2,1,0:T(8,128)(2,1)S(1)}, u32[]{:S(2)}, u32[]{:S(2)}) async-start(bf16[4,192,256]{2,1,0:T(8,128)(2,1)} %broadcast_in_dim.91), calls=%async_computation | async-start | bytes 786432 | tf_op jit(solution)/shard_map/all_to_all | solution.py:40
  15.4 3.7 %collective-permute-start = (f32[16,256]{1,0:T(8,128)S(1)}, f32[16,256]{1,0:T(8,128)S(1)}, u32[]{:S(2)}, u32[]{:S(2)}) collective-permute-start(f32[16,256]{1,0:T(8,128)S(1)} %broadcast_in_dim.92), channel_id=1, source_target_pairs={{0,32},{32,0},{1,33},{33,1},{2,34},{34,2},{3,35},{35,3},{4,36},{36... | collective-permute-start | bytes 49160 | tf_op jit(solution)/shard_map/ppermute | solution.py:209
  32.3 13.1 %collective-permute-start.1 = (bf16[4,192,256]{2,1,0:T(8,128)(2,1)S(1)}, bf16[4,192,256]{2,1,0:T(8,128)(2,1)S(1)}, u32[]{:S(2)}, u32[]{:S(2)}) collective-permute-start(bf16[4,192,256]{2,1,0:T(8,128)(2,1)S(1)} %all-to-all-done.near_ref), channel_id=1, source_target_pairs={{0,1},{1,0},{2,3},{3,2},{4,5},{5,4},{6,7},{7,6},{8,9},{9,8},{10,11... | collective-permute-start | bytes 1179656 | tf_op jit(solution)/shard_map/ppermute | solution.py:214
  45.4 5.5 %copy-start.6 = (bf16[512,256]{1,0:T(8,128)(2,1)S(1)}, bf16[512,256]{1,0:T(8,128)(2,1)}, u32[]{:S(2)}) copy-start(bf16[512,256]{1,0:T(8,128)(2,1)} %param.14) | copy-start | bytes 786436
  45.4 5.5 %copy-start.7 = (bf16[512,256]{1,0:T(8,128)(2,1)S(1)}, bf16[512,256]{1,0:T(8,128)(2,1)}, u32[]{:S(2)}) copy-start(bf16[512,256]{1,0:T(8,128)(2,1)} %param.13) | copy-start | bytes 786436
  46.2 28.0 %collective-permute-start.2 = (bf16[4,192,512]{2,1,0:T(8,128)(2,1)S(1)}, bf16[4,192,512]{2,1,0:T(8,128)(2,1)S(1)}, u32[]{:S(2)}, u32[]{:S(2)}) collective-permute-start(bf16[4,192,512]{2,1,0:T(8,128)(2,1)S(1)} %norm.1.own_ref), channel_id=1, source_target_pairs={{0,32},{32,0},{1,33},{33,1},{2,34},{34,2},{3,35},{35,3},{4,36},{36... | collective-permute-start | bytes 2359304 | tf_op jit(solution)/shard_map/ppermute | solution.py:226
  51.0 13.8 %collective-permute-start.3 = (bf16[512,384]{1,0:T(8,128)(2,1)S(1)}, bf16[512,384]{1,0:T(8,128)(2,1)S(1)}, u32[]{:S(2)}, u32[]{:S(2)}) collective-permute-start(bf16[512,384]{1,0:T(8,128)(2,1)S(1)} %pad_maximum_fusion.w0_ref), channel_id=1, source_target_pairs={{0,8},{8,16},{16,24},{24,0},{1,9},{9,17},{17,25},{25,1},{2,10},{10... | collective-permute-start | bytes 1179656 | tf_op jit(solution)/shard_map/ppermute | solution.py:200
  54.1 12.3 %collective-permute-start.4 = (bf16[512,384]{1,0:T(8,128)(2,1)S(1)}, bf16[512,384]{1,0:T(8,128)(2,1)S(1)}, u32[]{:S(2)}, u32[]{:S(2)}) collective-permute-start(bf16[512,384]{1,0:T(8,128)(2,1)S(1)} %pad_maximum_fusion.w0_ref), channel_id=1, source_target_pairs={{0,24},{8,0},{16,8},{24,16},{1,25},{9,1},{17,9},{25,17},{2,26},{10... | collective-permute-start | bytes 1179656 | tf_op jit(solution)/shard_map/ppermute | solution.py:200
  57.5 16.7 %collective-permute-start.5 = (bf16[512,384]{1,0:T(8,128)(2,1)S(1)}, bf16[512,384]{1,0:T(8,128)(2,1)S(1)}, u32[]{:S(2)}, u32[]{:S(2)}) collective-permute-start(bf16[512,384]{1,0:T(8,128)(2,1)S(1)} %pad_maximum_fusion.w0_ref), channel_id=1, source_target_pairs={{0,16},{8,24},{16,0},{24,8},{1,17},{9,25},{17,1},{25,9},{2,18},{10... | collective-permute-start | bytes 1179656 | tf_op jit(solution)/shard_map/ppermute | solution.py:200
  76.4 0.7 copy-start.1
  77.1 28.6 %all-to-all-start.1 = ((bf16[4,384,128]{2,1,0:T(8,128)(2,1)}), bf16[4,384,128]{2,1,0:T(8,128)(2,1)S(1)}, u32[]{:S(2)}, u32[]{:S(2)}) async-start(bf16[4,384,128]{2,1,0:T(8,128)(2,1)} %get-tuple-element.15), calls=%async_computation.1 | async-start | bytes 786432 | tf_op jit(solution)/shard_map/all_to_all | solution.py:239
  81.5 29.4 %copy-start.2 = (bf16[2,208,256]{2,1,0:T(8,128)(2,1)S(1)}, bf16[2,208,256]{2,1,0:T(8,128)(2,1)}, u32[]{:S(2)}) copy-start(bf16[2,208,256]{2,1,0:T(8,128)(2,1)} %copy-done.1) | copy-start | bytes 638980
  81.5 24.3 %collective-permute-start.6 = (bf16[2,208,256]{2,1,0:T(8,128)(2,1)}, bf16[2,208,256]{2,1,0:T(8,128)(2,1)S(1)}, u32[]{:S(2)}, u32[]{:S(2)}) collective-permute-start(bf16[2,208,256]{2,1,0:T(8,128)(2,1)} %copy-done.1), channel_id=1, source_target_pairs={{0,64},{1,65},{2,66},{3,67},{4,68},{5,69},{6,70},{7,71},{64,0},{65... | collective-permute-start | bytes 638984 | tf_op jit(solution)/shard_map/ppermute | solution.py:238
  106.8 28.5 %all-to-all-start.2 = ((bf16[4,2,208,256]{3,2,1,0:T(8,128)(2,1)}), bf16[4,2,208,256]{3,2,1,0:T(8,128)(2,1)S(1)}, u32[]{:S(2)}, u32[]{:S(2)}) async-start(bf16[4,2,208,256]{3,2,1,0:T(8,128)(2,1)} %broadcast_in_dim.100), calls=%async_computation.2 | async-start | bytes 1703936 | tf_op jit(solution)/shard_map/all_to_all | solution.py:40
  110.9 13.9 %collective-permute-start.7 = (bf16[2,208,256]{2,1,0:T(8,128)(2,1)S(1)}, bf16[2,208,256]{2,1,0:T(8,128)(2,1)S(1)}, u32[]{:S(2)}, u32[]{:S(2)}) collective-permute-start(bf16[2,208,256]{2,1,0:T(8,128)(2,1)S(1)} %copy-done.2), channel_id=1, source_target_pairs={{0,128},{128,256},{256,384},{384,0},{1,129},{129,257},{257,385},{3... | collective-permute-start | bytes 638984 | tf_op jit(solution)/shard_map/ppermute | solution.py:241
  114.3 10.6 %collective-permute-start.8 = (bf16[2,208,256]{2,1,0:T(8,128)(2,1)S(1)}, bf16[2,208,256]{2,1,0:T(8,128)(2,1)S(1)}, u32[]{:S(2)}, u32[]{:S(2)}) collective-permute-start(bf16[2,208,256]{2,1,0:T(8,128)(2,1)S(1)} %copy-done.2), channel_id=1, source_target_pairs={{0,384},{128,0},{256,128},{384,256},{1,385},{129,1},{257,129},{385... | collective-permute-start | bytes 638984 | tf_op jit(solution)/shard_map/ppermute | solution.py:241
  117.5 13.1 %collective-permute-start.9 = (bf16[2,208,256]{2,1,0:T(8,128)(2,1)S(1)}, bf16[2,208,256]{2,1,0:T(8,128)(2,1)S(1)}, u32[]{:S(2)}, u32[]{:S(2)}) collective-permute-start(bf16[2,208,256]{2,1,0:T(8,128)(2,1)S(1)} %copy-done.2), channel_id=1, source_target_pairs={{0,256},{128,384},{256,0},{384,128},{1,257},{129,385},{257,1},{385... | collective-permute-start | bytes 638984 | tf_op jit(solution)/shard_map/ppermute | solution.py:241
  135.3 13.6 %copy-start.5 = (bf16[512,256]{1,0:T(8,128)(2,1)S(1)}, bf16[512,256]{1,0:T(8,128)(2,1)}, u32[]{:S(2)}) copy-start(bf16[512,256]{1,0:T(8,128)(2,1)} %param.15) | copy-start | bytes 786436
  141.7 27.1 %all-to-all-start.3 = ((bf16[8,208,128]{2,1,0:T(8,128)(2,1)}), bf16[8,208,128]{2,1,0:T(8,128)(2,1)S(1)}, u32[]{:S(2)}, u32[]{:S(2)}) async-start(bf16[8,208,128]{2,1,0:T(8,128)(2,1)} %far.1), calls=%async_computation.3 | async-start | bytes 851968 | tf_op jit(solution)/shard_map/all_to_all | solution.py:277
  149.0 10.1 %collective-permute-start.13 = (bf16[256,256]{1,0:T(8,128)(2,1)S(1)}, bf16[256,256]{1,0:T(8,128)(2,1)S(1)}, u32[]{:S(2)}, u32[]{:S(2)}) collective-permute-start(bf16[256,256]{1,0:T(8,128)(2,1)S(1)} %get-tuple-element.22), channel_id=1, source_target_pairs={{0,1},{1,0},{2,3},{3,2},{4,5},{5,4},{6,7},{7,6},{8,9},{9,8},{10,11... | collective-permute-start | bytes 393224 | tf_op jit(solution)/shard_map/ppermute | solution.py:217
  159.1 23.2 %collective-permute-start.14 = (bf16[256,512]{1,0:T(8,128)(2,1)S(1)}, bf16[256,512]{1,0:T(8,128)(2,1)S(1)}, u32[]{:S(2)}, u32[]{:S(2)}) collective-permute-start(bf16[256,512]{1,0:T(8,128)(2,1)S(1)} %pad_maximum_fusion.1.w0_ref), channel_id=1, source_target_pairs={{0,8},{8,16},{16,24},{24,0},{1,9},{9,17},{17,25},{25,1},{2,10},{10... | collective-permute-start | bytes 786440 | tf_op jit(solution)/shard_map/ppermute | solution.py:275
  162.0 22.4 %collective-permute-start.15 = (bf16[256,512]{1,0:T(8,128)(2,1)S(1)}, bf16[256,512]{1,0:T(8,128)(2,1)S(1)}, u32[]{:S(2)}, u32[]{:S(2)}) collective-permute-start(bf16[256,512]{1,0:T(8,128)(2,1)S(1)} %pad_maximum_fusion.1.w0_ref), channel_id=1, source_target_pairs={{0,24},{8,0},{16,8},{24,16},{1,25},{9,1},{17,9},{25,17},{2,26},{10... | collective-permute-start | bytes 786440 | tf_op jit(solution)/shard_map/ppermute | solution.py:275
  165.6 18.7 %collective-permute-start.16 = (bf16[256,512]{1,0:T(8,128)(2,1)S(1)}, bf16[256,512]{1,0:T(8,128)(2,1)S(1)}, u32[]{:S(2)}, u32[]{:S(2)}) collective-permute-start(bf16[256,512]{1,0:T(8,128)(2,1)S(1)} %pad_maximum_fusion.1.w0_ref), channel_id=1, source_target_pairs={{0,16},{8,24},{16,0},{24,8},{1,17},{9,25},{17,1},{25,9},{2,18},{10... | collective-permute-start | bytes 786440 | tf_op jit(solution)/shard_map/ppermute | solution.py:276
  169.5 14.9 %collective-permute-start.10 = (bf16[192,256]{1,0:T(8,128)(2,1)S(1)}, bf16[192,256]{1,0:T(8,128)(2,1)S(1)}, u32[]{:S(2)}, u32[]{:S(2)}) collective-permute-start(bf16[192,256]{1,0:T(8,128)(2,1)S(1)} %pad_maximum_fusion.2.m0_ref), channel_id=1, source_target_pairs={{0,2},{2,0},{4,6},{6,4},{1,3},{3,1},{5,7},{7,5},{8,10},{10,8},{12,... | collective-permute-start | bytes 294920 | tf_op jit(solution)/shard_map/ppermute | solution.py:287
  171.4 26.4 %collective-permute-start.11 = (bf16[192,256]{1,0:T(8,128)(2,1)S(1)}, bf16[192,256]{1,0:T(8,128)(2,1)S(1)}, u32[]{:S(2)}, u32[]{:S(2)}) collective-permute-start(bf16[192,256]{1,0:T(8,128)(2,1)S(1)} %pad_maximum_fusion.2.m0_ref), channel_id=1, source_target_pairs={{0,4},{2,6},{4,0},{6,2},{1,5},{3,7},{5,1},{7,3},{8,12},{10,14},{12... | collective-permute-start | bytes 294920 | tf_op jit(solution)/shard_map/ppermute | solution.py:287
  182.3 15.5 %collective-permute-start.12 = (bf16[192,256]{1,0:T(8,128)(2,1)S(1)}, bf16[192,256]{1,0:T(8,128)(2,1)S(1)}, u32[]{:S(2)}, u32[]{:S(2)}) collective-permute-start(bf16[192,256]{1,0:T(8,128)(2,1)S(1)} %pad_maximum_fusion.2.m0_ref), channel_id=1, source_target_pairs={{0,6},{2,4},{4,2},{6,0},{1,7},{3,5},{5,3},{7,1},{8,14},{10,12},{12... | collective-permute-start | bytes 294920 | tf_op jit(solution)/shard_map/ppermute | solution.py:287
  198.9 5.4 %collective-permute-start.17 = (bf16[192,256]{1,0:T(8,128)(2,1)S(1)}, bf16[192,256]{1,0:T(8,128)(2,1)S(1)}, u32[]{:S(2)}, u32[]{:S(2)}) collective-permute-start(bf16[192,256]{1,0:T(8,128)(2,1)S(1)} %get-tuple-element.20), channel_id=1, source_target_pairs={{0,1},{1,0},{2,3},{3,2},{4,5},{5,4},{6,7},{7,6},{8,9},{9,8},{10,11... | collective-permute-start | bytes 294920 | tf_op jit(solution)/shard_map/ppermute | solution.py:300

commit v3 on v2

--- a/solution.py
+++ b/solution.py
@@ -129,46 +129,61 @@
     return best, over(second, total)
 
 
-def near_kernel(q_ref, k0_ref, k1_ref, k2_ref, k3_ref, acc_ref, stat_ref, s_ref):
-    width = q_ref.shape[0]
-    acc_ref[...] = jnp.zeros_like(acc_ref)
-    best, total = scan_keys(
-        q_ref[...],
-        (k0_ref, k1_ref, k2_ref, k3_ref),
-        s_ref,
-        acc_ref,
-        jnp.full((1, width), -1e30, F32),
-        jnp.zeros((1, width), F32),
-    )
-    stat_ref[0:1, :] = best
-    stat_ref[1:2, :] = total
-    stat_ref[2:8, :] = jnp.zeros((6, width), F32)
+def near_kernel(q_ref, k0_ref, k1_ref, acc_ref, stat_ref, s_ref):
+    width = s_ref.shape[1]
+
+    def part(i, carry):
+        acc_ref[i] = jnp.zeros(acc_ref.shape[1:], F32)
+        best, total = scan_keys(
+            q_ref[pl.ds(pl.multiple_of(i * width, width), width), :],
+            (k0_ref, k1_ref),
+            s_ref,
+            acc_ref.at[i],
+            jnp.full((1, width), -1e30, F32),
+            jnp.zeros((1, width), F32),
+        )
+        stat_ref[i, 0:1, :] = best
+        stat_ref[i, 1:2, :] = total
+        stat_ref[i, 2:8, :] = jnp.zeros((6, width), F32)
+        return carry
+
+    lax.fori_loop(0, 2, part, 0)
 
 
 def far_kernel(q_ref, kv_ref, part_ref, stat_ref, out_ref, s_ref, acc_ref):
-    width = q_ref.shape[0]
-    acc_ref[...] = part_ref[...]
-    best, total = scan_keys(
-        q_ref[...], (kv_ref,), s_ref, acc_ref, stat_ref[0:1, :], stat_ref[1:2, :]
-    )
-    mixed = (acc_ref[...] / total).T.astype(BF16)
-    level = best + jnp.log(total)
-    high = level.astype(BF16)
-    rest = level - high.astype(F32)
-    mid = rest.astype(BF16)
-    low = (rest - mid.astype(F32)).astype(BF16)
-    for x in range(width // (2 * ROWS)):
-        stats = []
-        for part in (high, mid, low):
-            for piece in range(3):
-                at = x * 2 * ROWS + piece * 128
-                stats.append(part[:, at : at + 128].astype(F32))
-        stats.append(jnp.zeros((7, 128), F32))
-        stats = jnp.concatenate(stats, axis=0).astype(BF16)
-        for c in range(2):
-            at = (2 * x + c) * ROWS
-            out_ref[2 * x + c, :ROWS, :] = mixed[at : at + ROWS, :]
-            out_ref[2 * x + c, ROWS : ROWS + 16, :] = stats
+    width = s_ref.shape[1]
+
+    def part(i, carry):
+        acc_ref[...] = part_ref[i]
+        best, total = scan_keys(
+            q_ref[pl.ds(pl.multiple_of(i * width, width), width), :],
+            (kv_ref,),
+            s_ref,
+            acc_ref,
+            stat_ref[i, 0:1, :],
+            stat_ref[i, 1:2, :],
+        )
+        mixed = (acc_ref[...] * (1.0 / total)).astype(BF16).T
+        level = best + jnp.log(total)
+        high = level.astype(BF16)
+        rest = level - high.astype(F32)
+        mid = rest.astype(BF16)
+        low = (rest - mid.astype(F32)).astype(BF16)
+        for x in range(width // (2 * ROWS)):
+            stats = []
+            for piece in (high, mid, low):
+                for third in range(3):
+                    at = x * 2 * ROWS + third * 128
+                    stats.append(piece[:, at : at + 128].astype(F32))
+            stats.append(jnp.zeros((7, 128), F32))
+            stats = jnp.concatenate(stats, axis=0).astype(BF16)
+            for c in range(2):
+                at = (2 * x + c) * ROWS
+                out_ref[i, 2 * x + c, :ROWS, :] = mixed[at : at + ROWS, :]
+                out_ref[i, 2 * x + c, ROWS : ROWS + 16, :] = stats
+        return carry
+
+    lax.fori_loop(0, 2, part, 0)
 
 
 def out_kernel(
@@ -205,7 +220,7 @@
     core = core.astype(jnp.int32)[None]
     parity = lax.axis_index("c0").astype(jnp.int32)[None]
 
-    live = jnp.full((16, 256), jnp.sum((visible >= 0).astype(F32)), F32)
+    live = jnp.full((8, 256), jnp.sum((visible >= 0).astype(F32)), F32)
     counts = jnp.stack([live, lax.ppermute(live, "core", ring(2, 1))])
 
     pos = embed(visible, 2048)
@@ -228,7 +243,7 @@
         qkv_kernel,
         out_shape=(
             jax.ShapeDtypeStruct((4, 2 * ROWS, 128), BF16),
-            jax.ShapeDtypeStruct((2, ROWS + 16, 256), BF16),
+            jax.ShapeDtypeStruct((2, ROWS + 8, 256), BF16),
         ),
         in_specs=[SMEM] * 2 + [VMEM] * 7,
         out_specs=(VMEM, VMEM),
@@ -237,33 +252,28 @@
     )(source, core, own, other, *weights, counts)
     far_kv = lax.ppermute(kv, ("zh", "c2", "c1", "c0"), ring(16, 8))
     query = lax.all_to_all(query, "row", 0, 0).reshape(8 * ROWS, 128)
-    near_kv = [kv[None]]
-    near_kv += [lax.ppermute(kv, "y", ring(4, s))[None] for s in SHIFTS[1:]]
+    beside = lax.ppermute(kv, "y", [(i, i ^ 1) for i in range(4)])
+    near_kv = jnp.stack([kv, beside])
+    across = lax.ppermute(near_kv, "y", [(i, i ^ 2) for i in range(4)])
+    near_kv = [near_kv, across]
     far_kv = spread(far_kv, "y", 4)
-    kv_spec = pl.BlockSpec((4, 2, ROWS + 16, 256), lambda i: (0, 0, 0, 0))
-    one_spec = pl.BlockSpec((1, 2, ROWS + 16, 256), lambda i: (0, 0, 0, 0))
-    q_spec = pl.BlockSpec((4 * ROWS, 128), lambda i: (i, 0))
-    acc_spec = pl.BlockSpec((128, 4 * ROWS), lambda i: (0, i))
-    stat_spec = pl.BlockSpec((8, 4 * ROWS), lambda i: (0, i))
     acc, stat = pl.pallas_call(
         near_kernel,
-        grid=(2,),
         out_shape=(
-            jax.ShapeDtypeStruct((128, 8 * ROWS), F32),
-            jax.ShapeDtypeStruct((8, 8 * ROWS), F32),
+            jax.ShapeDtypeStruct((2, 128, 4 * ROWS), F32),
+            jax.ShapeDtypeStruct((2, 8, 4 * ROWS), F32),
         ),
-        in_specs=[q_spec] + [one_spec] * 4,
-        out_specs=(acc_spec, stat_spec),
+        in_specs=[VMEM] * 3,
+        out_specs=(VMEM, VMEM),
         scratch_shapes=[pltpu.VMEM((8 * ROWS, 4 * ROWS), F32)],
         compiler_params=PARAMS,
         name="near",
     )(query, *near_kv)
     part = pl.pallas_call(
         far_kernel,
-        grid=(2,),
-        out_shape=jax.ShapeDtypeStruct((8, ROWS + 16, 128), BF16),
-        in_specs=[q_spec, kv_spec, acc_spec, stat_spec],
-        out_specs=pl.BlockSpec((4, ROWS + 16, 128), lambda i: (i, 0, 0)),
+        out_shape=jax.ShapeDtypeStruct((2, 4, ROWS + 16, 128), BF16),
+        in_specs=[VMEM] * 4,
+        out_specs=VMEM,
         scratch_shapes=[
             pltpu.VMEM((8 * ROWS, 4 * ROWS), F32),
             pltpu.VMEM((128, 4 * ROWS), F32),
@@ -271,6 +281,7 @@
         compiler_params=PARAMS,
         name="far",
     )(query, far_kv, acc, stat)
+    part = part.reshape(8, ROWS + 16, 128)
     outward = [jnp.concatenate([keep, taken], axis=1)]
     outward += [lax.ppermute(outward[0], "row", ring(4, s)) for s in SHIFTS[1:3]]
     outward.append(lax.ppermute(outward[0], "row", ring(4, SHIFTS[3])))
@@ -281,10 +292,9 @@
     share = share / jnp.sum(share, axis=0, keepdims=True)
     mixed = jnp.sum(part[:, :, :ROWS, :].astype(F32) * share[..., None], axis=0)
     mixed = jnp.concatenate([mixed[0], mixed[1]], axis=1).astype(BF16)
-    heads = [mixed]
-    for k in (1, 2, 3):
-        pairs = [(g, g ^ k) for g in range(4)]
-        heads.append(lax.ppermute(mixed, ("c2", "c1"), pairs))
+    heads = [mixed] + [None] * 3
+    for k in (3, 2, 1):
+        heads[k] = lax.ppermute(mixed, ("c2", "c1"), [(g, g ^ k) for g in range(4)])
     own, away = pl.pallas_call(
         out_kernel,
         out_shape=(

time: 206 us -> 204 us (level)
    ppermute x6 -> x5, waiting for transfers between devices: 22.8 us -> 27.5 us  [the longest x1 14 us: sublayer(): across = lax.ppermute(near_kv, 'y', [(i, i ^ 2) for i in range(4)])]
    ppermute x1, waiting for transfers between devices: 13.4 us -> 9.81 us  [sublayer(): far_kv = lax.ppermute(kv, ('zh', 'c2', 'c1', 'c0'), ring(16, 8))]
    ppermute x6 -> x5, starting transfers between devices: 25.1 us -> 22.9 us  [the longest x3 14.6 us: sublayer(): heads[k] = lax.ppermute(mixed, ('c2', 'c1'), [(g, g ^ k) for g in range(4)])]
  transfers between devices with their start and end apart: 22 -> 21, of which waited for: 12 -> 11; matrix products, arithmetic and copies ran while one was open for 5% -> 5% of each run, Pallas kernels for 2% -> 2%
where the time goes in v3:
time: 204 us; the launch traced here: 203 us
  starting transfers between devices  102 us (50%)
  waiting for transfers between devices  72.2 us (35%)
  Pallas kernels  15.1 us (7%)
  other arithmetic  8.94 us (4%)
  local copies, waits for them, and re-layouts  4.85 us (2%)
    all_to_all x2, starting transfers between devices, spread(): return lax.all_to_all(copies, axes, 0, 0)  15.9 us
    ppermute x3, starting transfers between devices, sublayer(): heads[k] = lax.ppermute(mixed, ('c2', 'c1'), [(g, g ^ k) for g in range(4)])  14.6 us
    ppermute x1, waiting for transfers between devices, sublayer(): across = lax.ppermute(near_kv, 'y', [(i, i ^ 2) for i in range(4)])  14 us
    ppermute x3, waiting for transfers between devices, sublayer(): heads[k] = lax.ppermute(mixed, ('c2', 'c1'), [(g, g ^ k) for g in range(4)])  13.5 us
    ppermute x3, waiting for transfers between devices, sublayer(): weights += [lax.ppermute(w_own, 'row', ring(4, s)) for s in SHIFTS[1:]]  13.1 us
    all_to_all x2, waiting for transfers between devices, spread(): return lax.all_to_all(copies, axes, 0, 0)  12.6 us
    ppermute x1, starting transfers between devices, sublayer(): far_kv = lax.ppermute(kv, ('zh', 'c2', 'c1', 'c0'), ring(16, 8))  10.7 us
    ppermute x3, starting transfers between devices, sublayer(): weights += [lax.ppermute(w_own, 'row', ring(4, s)) for s in SHIFTS[1:]]  9.93 us
  transfers between devices with their start and end apart: 21, of which 11 were waited for; matrix products, arithmetic and copies ran while one was open for 5% of the time, Pallas kernels for 2%

profile of v3, /device:TPU:1, one launch (start us, length us, event | category | flops | bytes accessed | tf_op | source)
XLA Modules:
  0.0 203.4 jit_solution(3855545925892077218)
XLA Ops:
  0.0 1.7 broadcast_in_dim.79
  1.7 11.7 %all-to-all-start = ((bf16[4,192,256]{2,1,0:T(8,128)(2,1)}), bf16[4,192,256]{2,1,0:T(8,128)(2,1)S(1)}, u32[]{:S(2)}, u32[]{:S(2)}) async-start(bf16[4,192,256]{2,1,0:T(8,128)(2,1)} %broadcast_in_dim.79), calls=%async_computation | async-start | bytes 786432 | tf_op jit(solution)/shard_map/all_to_all | solution.py:40
  13.4 1.3 fusion.17
  14.7 0.6 broadcast_in_dim.80
  15.4 2.9 %collective-permute-start = (f32[8,256]{1,0:T(8,128)S(1)}, f32[8,256]{1,0:T(8,128)S(1)}, u32[]{:S(2)}, u32[]{:S(2)}) collective-permute-start(f32[8,256]{1,0:T(8,128)S(1)} %broadcast_in_dim.80), channel_id=1, source_target_pairs={{0,32},{32,0},{1,33},{33,1},{2,34},{34,2},{3,35},{35,3},{4,36},{36... | collective-permute-start | bytes 24584 | tf_op jit(solution)/shard_map/ppermute | solution.py:224
  18.3 0.7 fusion.18
  19.0 0.1 collective-permute-done
  19.0 0.6 stack.80.cnt_ref
  19.7 12.6 %all-to-all-done.near_ref = bf16[4,192,256]{2,1,0:T(8,128)(2,1)S(1)} async-done(((bf16[4,192,256]{2,1,0:T(8,128)(2,1)}), bf16[4,192,256]{2,1,0:T(8,128)(2,1)S(1)}, u32[]{:S(2)}, u32[]{:S(2)}) %all-to-all-start) | async-done | bytes 393248 | tf_op jit(solution)/shard_map/all_to_all | solution.py:40
  32.3 5.7 %collective-permute-start.1 = (bf16[4,192,256]{2,1,0:T(8,128)(2,1)S(1)}, bf16[4,192,256]{2,1,0:T(8,128)(2,1)S(1)}, u32[]{:S(2)}, u32[]{:S(2)}) collective-permute-start(bf16[4,192,256]{2,1,0:T(8,128)(2,1)S(1)} %all-to-all-done.near_ref), channel_id=1, source_target_pairs={{0,1},{1,0},{2,3},{3,2},{4,5},{5,4},{6,7},{7,6},{8,9},{9,8},{10,11... | collective-permute-start | bytes 1179656 | tf_op jit(solution)/shard_map/ppermute | solution.py:229
  38.0 5.3 %add_sine_fusion.pos_ref = f32[192,2048]{1,0:T(8,128)S(1)} fusion(f32[2048]{0:T(1024)S(1)} %get-tuple-element.29, f32[2048]{0:T(1024)S(1)} %get-tuple-element.28, f32[192]{0:T(256)S(1)} %get-tuple-element.27, f32[192]{0:T(256)S(1)} %get-tuple-element.26, f32[192]{0:T(256)S(1)} %get-tuple-element.25, pred[2048]{0:T(1024)(128)(4,1)S(1)} %get-tuple-element.30, ...), kind=kLoop, calls=%fused_computation | loop fusion | flops 1572864 | bytes 1595648 | tf_op jit(solution)/shard_map/sin | solution.py:35
  43.4 2.0 collective-permute-done.1.side_ref
  45.4 0.8 norm.1.own_ref
  46.2 4.6 %collective-permute-start.2 = (bf16[4,192,512]{2,1,0:T(8,128)(2,1)S(1)}, bf16[4,192,512]{2,1,0:T(8,128)(2,1)S(1)}, u32[]{:S(2)}, u32[]{:S(2)}) collective-permute-start(bf16[4,192,512]{2,1,0:T(8,128)(2,1)S(1)} %norm.1.own_ref), channel_id=1, source_target_pairs={{0,32},{32,0},{1,33},{33,1},{2,34},{34,2},{3,35},{35,3},{4,36},{36... | collective-permute-start | bytes 2359304 | tf_op jit(solution)/shard_map/ppermute | solution.py:241
  50.9 0.1 pad_maximum_fusion.1.w0_ref
  51.0 3.1 %collective-permute-start.3 = (bf16[512,384]{1,0:T(8,128)(2,1)S(1)}, bf16[512,384]{1,0:T(8,128)(2,1)S(1)}, u32[]{:S(2)}, u32[]{:S(2)}) collective-permute-start(bf16[512,384]{1,0:T(8,128)(2,1)S(1)} %pad_maximum_fusion.1.w0_ref), channel_id=1, source_target_pairs={{0,8},{8,16},{16,24},{24,0},{1,9},{9,17},{17,25},{25,1},{2,10},{10... | collective-permute-start | bytes 1179656 | tf_op jit(solution)/shard_map/ppermute | solution.py:215
  54.1 3.4 %collective-permute-start.4 = (bf16[512,384]{1,0:T(8,128)(2,1)S(1)}, bf16[512,384]{1,0:T(8,128)(2,1)S(1)}, u32[]{:S(2)}, u32[]{:S(2)}) collective-permute-start(bf16[512,384]{1,0:T(8,128)(2,1)S(1)} %pad_maximum_fusion.1.w0_ref), channel_id=1, source_target_pairs={{0,24},{8,0},{16,8},{24,16},{1,25},{9,1},{17,9},{25,17},{2,26},{10... | collective-permute-start | bytes 1179656 | tf_op jit(solution)/shard_map/ppermute | solution.py:215
  57.5 3.4 %collective-permute-start.5 = (bf16[512,384]{1,0:T(8,128)(2,1)S(1)}, bf16[512,384]{1,0:T(8,128)(2,1)S(1)}, u32[]{:S(2)}, u32[]{:S(2)}) collective-permute-start(bf16[512,384]{1,0:T(8,128)(2,1)S(1)} %pad_maximum_fusion.1.w0_ref), channel_id=1, source_target_pairs={{0,16},{8,24},{16,0},{24,8},{1,17},{9,25},{17,1},{25,9},{2,18},{10... | collective-permute-start | bytes 1179656 | tf_op jit(solution)/shard_map/ppermute | solution.py:215
  61.0 0.1 pad_add_fusion.1.src_ref
  61.1 3.7 %collective-permute-done.3.w1_ref = bf16[512,384]{1,0:T(8,128)(2,1)S(1)} collective-permute-done((bf16[512,384]{1,0:T(8,128)(2,1)S(1)}, bf16[512,384]{1,0:T(8,128)(2,1)S(1)}, u32[]{:S(2)}, u32[]{:S(2)}) %collective-permute-start.3) | collective-permute-done | bytes 393248 | tf_op jit(solution)/shard_map/ppermute | solution.py:215
  64.8 1.6 collective-permute-done.4.w2_ref
  66.4 7.8 %collective-permute-done.5.w3_ref = bf16[512,384]{1,0:T(8,128)(2,1)S(1)} collective-permute-done((bf16[512,384]{1,0:T(8,128)(2,1)S(1)}, bf16[512,384]{1,0:T(8,128)(2,1)S(1)}, u32[]{:S(2)}, u32[]{:S(2)}) %collective-permute-start.5) | collective-permute-done | bytes 393248 | tf_op jit(solution)/shard_map/ppermute | solution.py:215
  74.2 0.0 collective-permute-done.2.oth_ref
  74.2 2.3 %qkv.1 = (bf16[4,384,128]{2,1,0:T(8,128)(2,1)}, bf16[2,200,256]{2,1,0:T(8,128)(2,1)S(1)}) custom-call(s32[4]{0:T(128)S(1)} %pad_add_fusion.1.src_ref, s32[1]{0:T(128)} %bitcast.12.core_ref, bf16[4,192,512]{2,1,0:T(8,128)(2,1)S(1)} %norm.1.own_ref, bf16[4,192,512]{2,1,0:T(8,128)(2,1)S(1)} %collective-permute-done.2.oth_ref, ...), custom_call_target="tpu_custom_call" | custom-call | tf_op jit(solution)/shard_map/qkv/pallas_call | solution.py:242
  76.4 0.7 copy-done.1
  77.1 4.5 %all-to-all-start.1 = ((bf16[4,384,128]{2,1,0:T(8,128)(2,1)}), bf16[4,384,128]{2,1,0:T(8,128)(2,1)S(1)}, u32[]{:S(2)}, u32[]{:S(2)}) async-start(bf16[4,384,128]{2,1,0:T(8,128)(2,1)} %get-tuple-element.15), calls=%async_computation.1 | async-start | bytes 786432 | tf_op jit(solution)/shard_map/all_to_all | solution.py:254
  81.6 10.7 %collective-permute-start.6 = (bf16[2,200,256]{2,1,0:T(8,128)(2,1)}, bf16[2,200,256]{2,1,0:T(8,128)(2,1)S(1)}, u32[]{:S(2)}, u32[]{:S(2)}) collective-permute-start(bf16[2,200,256]{2,1,0:T(8,128)(2,1)} %copy-done.1), channel_id=1, source_target_pairs={{0,64},{1,65},{2,66},{3,67},{4,68},{5,69},{6,70},{7,71},{64,0},{65... | collective-permute-start | bytes 614408 | tf_op jit(solution)/shard_map/ppermute | solution.py:253
  92.3 3.2 %collective-permute-start.7 = (bf16[2,200,256]{2,1,0:T(8,128)(2,1)}, bf16[2,200,256]{2,1,0:T(8,128)(2,1)S(1)}, u32[]{:S(2)}, u32[]{:S(2)}) collective-permute-start(bf16[2,200,256]{2,1,0:T(8,128)(2,1)} %copy-done.1), channel_id=1, source_target_pairs={{0,128},{128,0},{256,384},{384,256},{1,129},{129,1},{257,385},{385... | collective-permute-start | bytes 614408 | tf_op jit(solution)/shard_map/ppermute | solution.py:255
  95.5 9.8 %collective-permute-done.6 = bf16[2,200,256]{2,1,0:T(8,128)(2,1)S(1)} collective-permute-done((bf16[2,200,256]{2,1,0:T(8,128)(2,1)}, bf16[2,200,256]{2,1,0:T(8,128)(2,1)S(1)}, u32[]{:S(2)}, u32[]{:S(2)}) %collective-permute-start.6) | collective-permute-done | bytes 204832 | tf_op jit(solution)/shard_map/ppermute | solution.py:253
  105.3 0.0 all-to-all-done.1
  105.3 1.0 broadcast_in_dim.88
  106.3 4.2 %all-to-all-start.2 = ((bf16[4,2,200,256]{3,2,1,0:T(8,128)(2,1)}), bf16[4,2,200,256]{3,2,1,0:T(8,128)(2,1)S(1)}, u32[]{:S(2)}, u32[]{:S(2)}) async-start(bf16[4,2,200,256]{3,2,1,0:T(8,128)(2,1)} %broadcast_in_dim.88), calls=%async_computation.2 | async-start | bytes 1638400 | tf_op jit(solution)/shard_map/all_to_all | solution.py:40
  110.5 0.0 collective-permute-done.7
  110.5 5.0 %collective-permute-start.8 = (bf16[2,2,200,256]{3,2,1,0:T(8,128)(2,1)S(1)}, bf16[2,2,200,256]{3,2,1,0:T(8,128)(2,1)S(1)}, u32[]{:S(2)}, u32[]{:S(2)}) collective-permute-start(bf16[2,2,200,256]{3,2,1,0:T(8,128)(2,1)S(1)} %pad_maximum_fusion.k0_ref), channel_id=1, source_target_pairs={{0,256},{128,384},{256,0},{384,128},{1,257},{129,385},{257,1},{385... | collective-permute-start | bytes 1228808 | tf_op jit(solution)/shard_map/ppermute | solution.py:257
  115.6 14.0 %collective-permute-done.8.k1_ref = bf16[2,2,200,256]{3,2,1,0:T(8,128)(2,1)S(1)} collective-permute-done((bf16[2,2,200,256]{3,2,1,0:T(8,128)(2,1)S(1)}, bf16[2,2,200,256]{3,2,1,0:T(8,128)(2,1)S(1)}, u32[]{:S(2)}, u32[]{:S(2)}) %collective-permute-start.8) | collective-permute-done | bytes 409632 | tf_op jit(solution)/shard_map/ppermute | solution.py:257
  129.5 4.7 %near.1 = (f32[2,128,768]{2,1,0:T(8,128)S(1)}, f32[2,8,768]{2,1,0:T(8,128)S(1)}) custom-call(bf16[1536,128]{1,0:T(8,128)(2,1)S(1)} %bitcast.26, bf16[2,2,200,256]{3,2,1,0:T(8,128)(2,1)S(1)} %pad_maximum_fusion.k0_ref, bf16[2,2,200,256]{3,2,1,0:T(8,128)(2,1)S(1)} %collective-permute-done.8.k1_ref), custom_call_target="tpu_custom_call" | custom-call | tf_op jit(solution)/shard_map/near/pallas_call | solution.py:260
  134.2 0.0 all-to-all-done.2.kv_ref
  134.3 0.0 copy-start.5
  134.3 6.4 %far.1 = bf16[2,4,208,128]{3,2,1,0:T(8,128)(2,1)} custom-call(bf16[1536,128]{1,0:T(8,128)(2,1)S(1)} %bitcast.27, bf16[4,2,200,256]{3,2,1,0:T(8,128)(2,1)S(1)} %all-to-all-done.2.kv_ref, f32[2,128,768]{2,1,0:T(8,128)S(1)} %get-tuple-element.17.part_ref, f32[2,8,768]{2,1,0:T(8,128)S(1)} %get-tuple-element.18.stat_ref), custom_call_target="tpu_custom_call" | custom-call | tf_op jit(solution)/shard_map/far/pallas_call | solution.py:272
  140.6 7.3 %all-to-all-start.3 = ((bf16[8,208,128]{2,1,0:T(8,128)(2,1)}), bf16[8,208,128]{2,1,0:T(8,128)(2,1)S(1)}, u32[]{:S(2)}, u32[]{:S(2)}) async-start(bf16[8,208,128]{2,1,0:T(8,128)(2,1)} %bitcast.20), calls=%async_computation.3 | async-start | bytes 851968 | tf_op jit(solution)/shard_map/all_to_all | solution.py:288
  148.0 5.8 %collective-permute-start.12 = (bf16[256,256]{1,0:T(8,128)(2,1)S(1)}, bf16[256,256]{1,0:T(8,128)(2,1)S(1)}, u32[]{:S(2)}, u32[]{:S(2)}) collective-permute-start(bf16[256,256]{1,0:T(8,128)(2,1)S(1)} %get-tuple-element.22), channel_id=1, source_target_pairs={{0,1},{1,0},{2,3},{3,2},{4,5},{5,4},{6,7},{7,6},{8,9},{9,8},{10,11... | collective-permute-start | bytes 393224 | tf_op jit(solution)/shard_map/ppermute | solution.py:232
  153.9 0.1 stack.73.grp_ref
  154.0 3.7 %collective-permute-done.12 = bf16[256,256]{1,0:T(8,128)(2,1)S(1)} collective-permute-done((bf16[256,256]{1,0:T(8,128)(2,1)S(1)}, bf16[256,256]{1,0:T(8,128)(2,1)S(1)}, u32[]{:S(2)}, u32[]{:S(2)}) %collective-permute-start.12) | collective-permute-done | bytes 131104 | tf_op jit(solution)/shard_map/ppermute | solution.py:232
  157.7 2.9 %collective-permute-start.13 = (bf16[256,512]{1,0:T(8,128)(2,1)S(1)}, bf16[256,512]{1,0:T(8,128)(2,1)S(1)}, u32[]{:S(2)}, u32[]{:S(2)}) collective-permute-start(bf16[256,512]{1,0:T(8,128)(2,1)S(1)} %pad_maximum_fusion.2.w0_ref), channel_id=1, source_target_pairs={{0,8},{8,16},{16,24},{24,0},{1,9},{9,17},{17,25},{25,1},{2,10},{10... | collective-permute-start | bytes 786440 | tf_op jit(solution)/shard_map/ppermute | solution.py:286
  160.6 3.6 %collective-permute-start.14 = (bf16[256,512]{1,0:T(8,128)(2,1)S(1)}, bf16[256,512]{1,0:T(8,128)(2,1)S(1)}, u32[]{:S(2)}, u32[]{:S(2)}) collective-permute-start(bf16[256,512]{1,0:T(8,128)(2,1)S(1)} %pad_maximum_fusion.2.w0_ref), channel_id=1, source_target_pairs={{0,24},{8,0},{16,8},{24,16},{1,25},{9,1},{17,9},{25,17},{2,26},{10... | collective-permute-start | bytes 786440 | tf_op jit(solution)/shard_map/ppermute | solution.py:286
  164.2 3.2 %collective-permute-start.15 = (bf16[256,512]{1,0:T(8,128)(2,1)S(1)}, bf16[256,512]{1,0:T(8,128)(2,1)S(1)}, u32[]{:S(2)}, u32[]{:S(2)}) collective-permute-start(bf16[256,512]{1,0:T(8,128)(2,1)S(1)} %pad_maximum_fusion.2.w0_ref), channel_id=1, source_target_pairs={{0,16},{8,24},{16,0},{24,8},{1,17},{9,25},{17,1},{25,9},{2,18},{10... | collective-permute-start | bytes 786440 | tf_op jit(solution)/shard_map/ppermute | solution.py:287
  167.4 0.0 all-to-all-done.3
  167.5 0.1 dynamic-slice_reduce_fusion
  167.6 0.1 fusion.16
  167.7 0.1 broadcast_divide_fusion
  167.8 0.3 multiply_reduce_fusion
  168.1 1.9 collective-permute-start.9
  170.0 10.8 %collective-permute-start.10 = (bf16[192,256]{1,0:T(8,128)(2,1)S(1)}, bf16[192,256]{1,0:T(8,128)(2,1)S(1)}, u32[]{:S(2)}, u32[]{:S(2)}) collective-permute-start(bf16[192,256]{1,0:T(8,128)(2,1)S(1)} %pad_maximum_fusion.3.m0_ref), channel_id=1, source_target_pairs={{0,4},{2,6},{4,0},{6,2},{1,5},{3,7},{5,1},{7,3},{8,12},{10,14},{12... | collective-permute-start | bytes 294920 | tf_op jit(solution)/shard_map/ppermute | solution.py:297
  180.8 0.0 collective-permute-done.13.w1_ref
  180.8 1.9 collective-permute-start.11
  182.7 0.1 pad_add_fusion.src_ref
  182.8 0.0 collective-permute-done.14.w2_ref
  182.8 0.0 collective-permute-done.15.w3_ref
  182.8 0.0 collective-permute-done.9.m1_ref
  182.8 13.5 %collective-permute-done.10.m2_ref = bf16[192,256]{1,0:T(8,128)(2,1)S(1)} collective-permute-done((bf16[192,256]{1,0:T(8,128)(2,1)S(1)}, bf16[192,256]{1,0:T(8,128)(2,1)S(1)}, u32[]{:S(2)}, u32[]{:S(2)}) %collective-permute-start.10) | collective-permute-done | bytes 98336 | tf_op jit(solution)/shard_map/ppermute | solution.py:297
  196.3 1.0 out.1
  197.3 1.9 collective-permute-start.16
  199.3 3.4 %collective-permute-done.16 = bf16[192,256]{1,0:T(8,128)(2,1)S(1)} collective-permute-done((bf16[192,256]{1,0:T(8,128)(2,1)S(1)}, bf16[192,256]{1,0:T(8,128)(2,1)S(1)}, u32[]{:S(2)}, u32[]{:S(2)}) %collective-permute-start.16) | collective-permute-done | bytes 98336 | tf_op jit(solution)/shard_map/ppermute | solution.py:310
  202.7 0.7 convert_add_fusion
  (27 shorter events, 0.3 us)
Async XLA Ops:
  0.0 50.8 %copy-start = (bf16[512,256]{1,0:T(8,128)(2,1)S(1)}, bf16[512,256]{1,0:T(8,128)(2,1)}, u32[]{:S(2)}) copy-start(bf16[512,256]{1,0:T(8,128)(2,1)} %param.12) | copy-start | bytes 786436
  0.0 45.4 %copy-start.3 = (f32[2048]{0:T(1024)S(1)}, f32[2048]{0:T(1024)}, u32[]{:S(2)}) copy-start(f32[2048]{0:T(1024)} %param.10) | copy-start | bytes 24580
  0.0 45.4 %copy-start.4 = (f32[2048]{0:T(1024)S(1)}, f32[2048]{0:T(1024)}, u32[]{:S(2)}) copy-start(f32[2048]{0:T(1024)} %param.11) | copy-start | bytes 24580
  1.7 30.6 %all-to-all-start = ((bf16[4,192,256]{2,1,0:T(8,128)(2,1)}), bf16[4,192,256]{2,1,0:T(8,128)(2,1)S(1)}, u32[]{:S(2)}, u32[]{:S(2)}) async-start(bf16[4,192,256]{2,1,0:T(8,128)(2,1)} %broadcast_in_dim.79), calls=%async_computation | async-start | bytes 786432 | tf_op jit(solution)/shard_map/all_to_all | solution.py:40
  15.4 3.7 %collective-permute-start = (f32[8,256]{1,0:T(8,128)S(1)}, f32[8,256]{1,0:T(8,128)S(1)}, u32[]{:S(2)}, u32[]{:S(2)}) collective-permute-start(f32[8,256]{1,0:T(8,128)S(1)} %broadcast_in_dim.80), channel_id=1, source_target_pairs={{0,32},{32,0},{1,33},{33,1},{2,34},{34,2},{3,35},{35,3},{4,36},{36... | collective-permute-start | bytes 24584 | tf_op jit(solution)/shard_map/ppermute | solution.py:224
  32.3 13.1 %collective-permute-start.1 = (bf16[4,192,256]{2,1,0:T(8,128)(2,1)S(1)}, bf16[4,192,256]{2,1,0:T(8,128)(2,1)S(1)}, u32[]{:S(2)}, u32[]{:S(2)}) collective-permute-start(bf16[4,192,256]{2,1,0:T(8,128)(2,1)S(1)} %all-to-all-done.near_ref), channel_id=1, source_target_pairs={{0,1},{1,0},{2,3},{3,2},{4,5},{5,4},{6,7},{7,6},{8,9},{9,8},{10,11... | collective-permute-start | bytes 1179656 | tf_op jit(solution)/shard_map/ppermute | solution.py:229
  45.4 5.5 %copy-start.6 = (bf16[512,256]{1,0:T(8,128)(2,1)S(1)}, bf16[512,256]{1,0:T(8,128)(2,1)}, u32[]{:S(2)}) copy-start(bf16[512,256]{1,0:T(8,128)(2,1)} %param.14) | copy-start | bytes 786436
  45.4 5.5 %copy-start.7 = (bf16[512,256]{1,0:T(8,128)(2,1)S(1)}, bf16[512,256]{1,0:T(8,128)(2,1)}, u32[]{:S(2)}) copy-start(bf16[512,256]{1,0:T(8,128)(2,1)} %param.13) | copy-start | bytes 786436
  46.2 28.0 %collective-permute-start.2 = (bf16[4,192,512]{2,1,0:T(8,128)(2,1)S(1)}, bf16[4,192,512]{2,1,0:T(8,128)(2,1)S(1)}, u32[]{:S(2)}, u32[]{:S(2)}) collective-permute-start(bf16[4,192,512]{2,1,0:T(8,128)(2,1)S(1)} %norm.1.own_ref), channel_id=1, source_target_pairs={{0,32},{32,0},{1,33},{33,1},{2,34},{34,2},{3,35},{35,3},{4,36},{36... | collective-permute-start | bytes 2359304 | tf_op jit(solution)/shard_map/ppermute | solution.py:241
  51.0 13.8 %collective-permute-start.3 = (bf16[512,384]{1,0:T(8,128)(2,1)S(1)}, bf16[512,384]{1,0:T(8,128)(2,1)S(1)}, u32[]{:S(2)}, u32[]{:S(2)}) collective-permute-start(bf16[512,384]{1,0:T(8,128)(2,1)S(1)} %pad_maximum_fusion.1.w0_ref), channel_id=1, source_target_pairs={{0,8},{8,16},{16,24},{24,0},{1,9},{9,17},{17,25},{25,1},{2,10},{10... | collective-permute-start | bytes 1179656 | tf_op jit(solution)/shard_map/ppermute | solution.py:215
  54.1 12.3 %collective-permute-start.4 = (bf16[512,384]{1,0:T(8,128)(2,1)S(1)}, bf16[512,384]{1,0:T(8,128)(2,1)S(1)}, u32[]{:S(2)}, u32[]{:S(2)}) collective-permute-start(bf16[512,384]{1,0:T(8,128)(2,1)S(1)} %pad_maximum_fusion.1.w0_ref), channel_id=1, source_target_pairs={{0,24},{8,0},{16,8},{24,16},{1,25},{9,1},{17,9},{25,17},{2,26},{10... | collective-permute-start | bytes 1179656 | tf_op jit(solution)/shard_map/ppermute | solution.py:215
  57.5 16.7 %collective-permute-start.5 = (bf16[512,384]{1,0:T(8,128)(2,1)S(1)}, bf16[512,384]{1,0:T(8,128)(2,1)S(1)}, u32[]{:S(2)}, u32[]{:S(2)}) collective-permute-start(bf16[512,384]{1,0:T(8,128)(2,1)S(1)} %pad_maximum_fusion.1.w0_ref), channel_id=1, source_target_pairs={{0,16},{8,24},{16,0},{24,8},{1,17},{9,25},{17,1},{25,9},{2,18},{10... | collective-permute-start | bytes 1179656 | tf_op jit(solution)/shard_map/ppermute | solution.py:215
  76.4 0.7 copy-start.1
  77.1 33.4 %copy-start.2 = (bf16[2,200,256]{2,1,0:T(8,128)(2,1)S(1)}, bf16[2,200,256]{2,1,0:T(8,128)(2,1)}, u32[]{:S(2)}) copy-start(bf16[2,200,256]{2,1,0:T(8,128)(2,1)} %copy-done.1) | copy-start | bytes 614404
  77.1 28.2 %all-to-all-start.1 = ((bf16[4,384,128]{2,1,0:T(8,128)(2,1)}), bf16[4,384,128]{2,1,0:T(8,128)(2,1)S(1)}, u32[]{:S(2)}, u32[]{:S(2)}) async-start(bf16[4,384,128]{2,1,0:T(8,128)(2,1)} %get-tuple-element.15), calls=%async_computation.1 | async-start | bytes 786432 | tf_op jit(solution)/shard_map/all_to_all | solution.py:254
  81.6 23.7 %collective-permute-start.6 = (bf16[2,200,256]{2,1,0:T(8,128)(2,1)}, bf16[2,200,256]{2,1,0:T(8,128)(2,1)S(1)}, u32[]{:S(2)}, u32[]{:S(2)}) collective-permute-start(bf16[2,200,256]{2,1,0:T(8,128)(2,1)} %copy-done.1), channel_id=1, source_target_pairs={{0,64},{1,65},{2,66},{3,67},{4,68},{5,69},{6,70},{7,71},{64,0},{65... | collective-permute-start | bytes 614408 | tf_op jit(solution)/shard_map/ppermute | solution.py:253
  92.3 18.2 %collective-permute-start.7 = (bf16[2,200,256]{2,1,0:T(8,128)(2,1)}, bf16[2,200,256]{2,1,0:T(8,128)(2,1)S(1)}, u32[]{:S(2)}, u32[]{:S(2)}) collective-permute-start(bf16[2,200,256]{2,1,0:T(8,128)(2,1)} %copy-done.1), channel_id=1, source_target_pairs={{0,128},{128,0},{256,384},{384,256},{1,129},{129,1},{257,385},{385... | collective-permute-start | bytes 614408 | tf_op jit(solution)/shard_map/ppermute | solution.py:255
  106.3 28.0 %all-to-all-start.2 = ((bf16[4,2,200,256]{3,2,1,0:T(8,128)(2,1)}), bf16[4,2,200,256]{3,2,1,0:T(8,128)(2,1)S(1)}, u32[]{:S(2)}, u32[]{:S(2)}) async-start(bf16[4,2,200,256]{3,2,1,0:T(8,128)(2,1)} %broadcast_in_dim.88), calls=%async_computation.2 | async-start | bytes 1638400 | tf_op jit(solution)/shard_map/all_to_all | solution.py:40
  110.5 19.0 %collective-permute-start.8 = (bf16[2,2,200,256]{3,2,1,0:T(8,128)(2,1)S(1)}, bf16[2,2,200,256]{3,2,1,0:T(8,128)(2,1)S(1)}, u32[]{:S(2)}, u32[]{:S(2)}) collective-permute-start(bf16[2,2,200,256]{3,2,1,0:T(8,128)(2,1)S(1)} %pad_maximum_fusion.k0_ref), channel_id=1, source_target_pairs={{0,256},{128,384},{256,0},{384,128},{1,257},{129,385},{257,1},{385... | collective-permute-start | bytes 1228808 | tf_op jit(solution)/shard_map/ppermute | solution.py:257
  134.3 13.7 %copy-start.5 = (bf16[512,256]{1,0:T(8,128)(2,1)S(1)}, bf16[512,256]{1,0:T(8,128)(2,1)}, u32[]{:S(2)}) copy-start(bf16[512,256]{1,0:T(8,128)(2,1)} %param.15) | copy-start | bytes 786436
  140.6 26.8 %all-to-all-start.3 = ((bf16[8,208,128]{2,1,0:T(8,128)(2,1)}), bf16[8,208,128]{2,1,0:T(8,128)(2,1)S(1)}, u32[]{:S(2)}, u32[]{:S(2)}) async-start(bf16[8,208,128]{2,1,0:T(8,128)(2,1)} %bitcast.20), calls=%async_computation.3 | async-start | bytes 851968 | tf_op jit(solution)/shard_map/all_to_all | solution.py:288
  148.0 9.7 %collective-permute-start.12 = (bf16[256,256]{1,0:T(8,128)(2,1)S(1)}, bf16[256,256]{1,0:T(8,128)(2,1)S(1)}, u32[]{:S(2)}, u32[]{:S(2)}) collective-permute-start(bf16[256,256]{1,0:T(8,128)(2,1)S(1)} %get-tuple-element.22), channel_id=1, source_target_pairs={{0,1},{1,0},{2,3},{3,2},{4,5},{5,4},{6,7},{7,6},{8,9},{9,8},{10,11... | collective-permute-start | bytes 393224 | tf_op jit(solution)/shard_map/ppermute | solution.py:232
  157.7 23.1 %collective-permute-start.13 = (bf16[256,512]{1,0:T(8,128)(2,1)S(1)}, bf16[256,512]{1,0:T(8,128)(2,1)S(1)}, u32[]{:S(2)}, u32[]{:S(2)}) collective-permute-start(bf16[256,512]{1,0:T(8,128)(2,1)S(1)} %pad_maximum_fusion.2.w0_ref), channel_id=1, source_target_pairs={{0,8},{8,16},{16,24},{24,0},{1,9},{9,17},{17,25},{25,1},{2,10},{10... | collective-permute-start | bytes 786440 | tf_op jit(solution)/shard_map/ppermute | solution.py:286
  160.6 22.2 %collective-permute-start.14 = (bf16[256,512]{1,0:T(8,128)(2,1)S(1)}, bf16[256,512]{1,0:T(8,128)(2,1)S(1)}, u32[]{:S(2)}, u32[]{:S(2)}) collective-permute-start(bf16[256,512]{1,0:T(8,128)(2,1)S(1)} %pad_maximum_fusion.2.w0_ref), channel_id=1, source_target_pairs={{0,24},{8,0},{16,8},{24,16},{1,25},{9,1},{17,9},{25,17},{2,26},{10... | collective-permute-start | bytes 786440 | tf_op jit(solution)/shard_map/ppermute | solution.py:286
  164.2 18.6 %collective-permute-start.15 = (bf16[256,512]{1,0:T(8,128)(2,1)S(1)}, bf16[256,512]{1,0:T(8,128)(2,1)S(1)}, u32[]{:S(2)}, u32[]{:S(2)}) collective-permute-start(bf16[256,512]{1,0:T(8,128)(2,1)S(1)} %pad_maximum_fusion.2.w0_ref), channel_id=1, source_target_pairs={{0,16},{8,24},{16,0},{24,8},{1,17},{9,25},{17,1},{25,9},{2,18},{10... | collective-permute-start | bytes 786440 | tf_op jit(solution)/shard_map/ppermute | solution.py:287
  168.1 14.7 %collective-permute-start.9 = (bf16[192,256]{1,0:T(8,128)(2,1)S(1)}, bf16[192,256]{1,0:T(8,128)(2,1)S(1)}, u32[]{:S(2)}, u32[]{:S(2)}) collective-permute-start(bf16[192,256]{1,0:T(8,128)(2,1)S(1)} %pad_maximum_fusion.3.m0_ref), channel_id=1, source_target_pairs={{0,2},{2,0},{4,6},{6,4},{1,3},{3,1},{5,7},{7,5},{8,10},{10,8},{12,... | collective-permute-start | bytes 294920 | tf_op jit(solution)/shard_map/ppermute | solution.py:297
  170.0 26.3 %collective-permute-start.10 = (bf16[192,256]{1,0:T(8,128)(2,1)S(1)}, bf16[192,256]{1,0:T(8,128)(2,1)S(1)}, u32[]{:S(2)}, u32[]{:S(2)}) collective-permute-start(bf16[192,256]{1,0:T(8,128)(2,1)S(1)} %pad_maximum_fusion.3.m0_ref), channel_id=1, source_target_pairs={{0,4},{2,6},{4,0},{6,2},{1,5},{3,7},{5,1},{7,3},{8,12},{10,14},{12... | collective-permute-start | bytes 294920 | tf_op jit(solution)/shard_map/ppermute | solution.py:297
  180.8 15.5 %collective-permute-start.11 = (bf16[192,256]{1,0:T(8,128)(2,1)S(1)}, bf16[192,256]{1,0:T(8,128)(2,1)S(1)}, u32[]{:S(2)}, u32[]{:S(2)}) collective-permute-start(bf16[192,256]{1,0:T(8,128)(2,1)S(1)} %pad_maximum_fusion.3.m0_ref), channel_id=1, source_target_pairs={{0,6},{2,4},{4,2},{6,0},{1,7},{3,5},{5,3},{7,1},{8,14},{10,12},{12... | collective-permute-start | bytes 294920 | tf_op jit(solution)/shard_map/ppermute | solution.py:297
  197.3 5.4 %collective-permute-start.16 = (bf16[192,256]{1,0:T(8,128)(2,1)S(1)}, bf16[192,256]{1,0:T(8,128)(2,1)S(1)}, u32[]{:S(2)}, u32[]{:S(2)}) collective-permute-start(bf16[192,256]{1,0:T(8,128)(2,1)S(1)} %get-tuple-element.20), channel_id=1, source_target_pairs={{0,1},{1,0},{2,3},{3,2},{4,5},{5,4},{6,7},{7,6},{8,9},{9,8},{10,11... | collective-permute-start | bytes 294920 | tf_op jit(solution)/shard_map/ppermute | solution.py:310
